TPU v7x, 512 devices: a whole 4x4x16 slice. The times are simulated.
512 devices in a mesh: lon: 64 (over x_hi, z, core), tp: 8 (over y, x_lo).
Axes of the slice: x: 4 (x_hi: 2, x_lo: 2; x = x_hi * 2 + x_lo), y: 4, z: 16, core: 2. Of those that a mesh axis runs over, the one named last changes fastest.
Arguments:
- image_tokens: bfloat16 [16384, 3072], P('lon', 'tp'), may hold values from -6 to 6
- style_tokens: bfloat16 [2048, 3072], P('lon', 'tp'), may hold values from -6 to 6
- qkv_weight: bfloat16 [3, 3072, 2048], P(None, 'lon', 'tp'), may hold values from -0.109375 to 0.109375
- out_weight: bfloat16 [2048, 3072], P('tp', 'lon'), may hold values from -0.125 to 0.125
- query_gain: float32 [128], replicated, may hold values from 0.6 to 9, as said below
- key_gain: float32 [128], replicated, may hold values from 0.6 to 9, as said below
- attend_flags: int32 [64, 1], P('lon'), may hold values from 0 to 1
Outputs:
- mixed: bfloat16 [16384, 3072], P('lon', 'tp')
Inputs may be any that keep to these rules, and one draw needn't show every extreme that they name: `query_gain`: positive gains. `key_gain`: positive gains.
All inputs are finite; a program needn't handle non-finite values.
Results may differ from a plain program's by a relative error of at most 0.015.
The roundings to bfloat16 on the way count: a program that leaves them out, or rounds other values in their place, can miss the bound.
Values may be sent and summed in bfloat16 or wider, within the bound.
No kernel may reach another device: no remote copies, remote signals or barrier semaphores. Data moves between devices by JAX's collectives and lax.ppermute only.
A program may use at most 64 MiB of HBM per device.

v0:
```python
import math

import jax
import jax.numpy as jnp
from jax import lax
from jax.sharding import PartitionSpec as P

HEAD = 128


def with_halo(block, sides, width):
    for axis, dim in sides:
        count = lax.axis_size(axis)
        forward = [(i, i + 1) for i in range(count - 1)]
        forward.append((count - 1, 0))
        backward = [(target, source) for source, target in forward]
        low = lax.ppermute(
            lax.slice_in_dim(block, block.shape[dim] - width, None, axis=dim), axis, forward
        )
        high = lax.ppermute(lax.slice_in_dim(block, 0, width, axis=dim), axis, backward)
        block = jnp.concatenate([low, block, high], axis=dim)
    return block


def head_norm(values, gain):
    return values * lax.rsqrt(jnp.mean(values * values, axis=-1, keepdims=True) + 1e-06) * gain


def local(image_tokens, style_tokens, qkv_weight, out_weight, query_gain, key_gain, attend_flags):
    count = image_tokens.shape[0]
    ref_local = style_tokens.shape[0]
    width_here = qkv_weight.shape[2]
    heads_here = width_here // HEAD
    image_full, style_full = (
        lax.all_gather(image_tokens, "tp", axis=1, tiled=True),
        lax.all_gather(style_tokens, "tp", axis=1, tiled=True),
    )
    panel = lax.all_gather(qkv_weight, "lon", axis=1, tiled=True)
    projected = jnp.einsum("td,jdc->jtc", image_full, panel, preferred_element_type=jnp.float32)
    style_proj = jnp.einsum(
        "td,jdc->jtc", style_full, panel[1:], preferred_element_type=jnp.float32
    )
    query = head_norm(projected[0].reshape(count, heads_here, HEAD), query_gain).astype(
        jnp.bfloat16
    )
    keys = head_norm(projected[1].reshape(count, heads_here, HEAD), key_gain).astype(jnp.bfloat16)
    values = projected[2].astype(jnp.bfloat16)
    own_pair = jnp.stack([keys.reshape(count, width_here), values])
    style_key = head_norm(style_proj[0].reshape(ref_local, heads_here, HEAD), key_gain).astype(
        jnp.bfloat16
    )
    style_pair = jnp.stack(
        [style_key.reshape(ref_local, width_here), style_proj[1].astype(jnp.bfloat16)]
    )
    widened = with_halo(own_pair, (("lon", 1),), count)
    style_all = lax.all_gather(style_pair, "lon", axis=1, tiled=True)
    ref_total = style_all.shape[1]
    key_set = jnp.concatenate([widened[0], style_all[0]], axis=0).reshape(-1, heads_here, HEAD)
    value_set = jnp.concatenate([widened[1], style_all[1]], axis=0).reshape(-1, heads_here, HEAD)
    flags = attend_flags[0]
    allowed = jnp.concatenate([jnp.ones((3 * count,), bool), jnp.full((ref_total,), flags[0] > 0)])
    scores = jnp.einsum(
        "qhe,khe->hqk", query, key_set, preferred_element_type=jnp.float32
    ) / math.sqrt(HEAD)
    scores = jnp.where(allowed[None, None, :], scores, -1e30)
    peak = jnp.max(scores, axis=-1, keepdims=True)
    expo = jnp.exp(scores - peak)
    weights = (expo / jnp.sum(expo, axis=-1, keepdims=True)).astype(jnp.bfloat16)
    attended = jnp.einsum("hqk,khe->qhe", weights, value_set, preferred_element_type=jnp.float32)
    attended = attended.astype(jnp.bfloat16).reshape(count, width_here)
    partial_sums = jnp.dot(
        attended,
        lax.all_gather(out_weight, "lon", axis=1, tiled=True),
        preferred_element_type=jnp.float32,
    )
    return lax.psum_scatter(
        partial_sums.astype(jnp.bfloat16), "tp", scatter_dimension=1, tiled=True
    )


def solution(mesh):
    in_specs = (
        P("lon", "tp"),
        P("lon", "tp"),
        P(None, "lon", "tp"),
        P("tp", "lon"),
        P(),
        P(),
        P("lon", None),
    )
    out_specs = P("lon", "tp")
    return jax.shard_map(local, mesh=mesh, in_specs=in_specs, out_specs=out_specs, check_vma=False)
```

profile of v0, /device:TPU:1, one launch (start us, length us, event | category | flops | bytes accessed | tf_op | source)
XLA Modules:
  0.0 558.2 jit_solution(1388387816739519293)
XLA Ops:
  6.5 0.0 copy-start
  6.5 0.0 all-gather.5.cloned.1.call-start
  6.5 0.7 all-gather.5.cloned.1.call-update
  7.3 0.0 all-gather.7.cloned.1.call-start
  7.3 0.7 all-gather.7.cloned.1.call-update
  8.0 0.0 all-gather.9.cloned.1.call-start
  8.1 23.5 %all_gather.17 = bf16[32,3072]{1,0:T(8,128)(2,1)S(1)} all-gather(bf16[32,384]{1,0:T(8,128)(2,1)} %param.8), channel_id=1, replica_groups=mesh['lon'=64,'tp'=8] {'tp'}, dimensions={1}, use_global_device_ids=true | all-gather | bytes 221184 | tf_op jit(solution)/shard_map/all_gather | solution.py:36
  31.6 0.0 copy-done
  31.6 137.2 %all-gather.5.cloned.1.call-done = bf16[3,3072,256]{2,1,0:T(8,128)(2,1)} async-done(((bf16[3,48,256]{2,1,0:T(8,128)(2,1)}), bf16[3,3072,256]{2,1,0:T(8,128)(2,1)}) %all-gather.5.cloned.1.call-update) | async-done | bytes 4718608 | tf_op jit(solution)/shard_map/all_gather | solution.py:38
  168.8 2.5 fusion.23
  171.3 0.1 reduce_sum.37
  171.5 0.1 mul.98
  171.6 0.6 pad_maximum_fusion.2
  172.3 0.0 all-gather.9.cloned.1.call-update
  172.3 0.0 all-gather.11.cloned.1.call-start
  172.3 0.5 all-gather.11.cloned.1.call-update
  172.9 0.0 reduce-scatter.4.cloned.1.call-start
  173.6 39.7 %all-gather.7.cloned.1.call-done = bf16[256,3072]{1,0:T(8,128)(2,1)} async-done(((bf16[256,384]{1,0:T(8,128)(2,1)}), bf16[256,3072]{1,0:T(8,128)(2,1)}) %all-gather.7.cloned.1.call-update) | async-done | bytes 1572880 | tf_op jit(solution)/shard_map/all_gather | solution.py:35
  213.2 4.3 fusion.17
  217.6 0.1 fusion.43
  217.8 6.8 %collective-permute-start = (bf16[2,256,256]{1,2,0:T(8,128)(2,1)S(1)}, bf16[2,256,256]{1,2,0:T(8,128)(2,1)S(1)}, u32[]{:S(2)}, u32[]{:S(2)}) collective-permute-start(bf16[2,256,256]{1,2,0:T(8,128)(2,1)S(1)} %pad_maximum_fusion.1), channel_id=1, source_target_pairs={{0,8},{8,16},{16,24},{24,32},{32,40},{40,48},{48,56},{56,64},{64,7... | collective-permute-start | bytes 786440 | tf_op jit(solution)/shard_map/ppermute | solution.py:17
  224.6 1.9 collective-permute-start.1
  226.6 0.9 copy.13
  227.4 0.5 collective-permute-done
  227.9 4.5 collective-permute-done.1
  232.4 0.1 pad_maximum_fusion
  232.5 0.8 fusion.42
  233.3 0.2 copy.14
  233.6 130.2 %all-gather.9.cloned.1.call-done = bf16[2,2048,256]{2,1,0:T(8,128)(2,1)} async-done(((bf16[2,32,256]{2,1,0:T(8,128)(2,1)}), bf16[2,2048,256]{2,1,0:T(8,128)(2,1)}) %all-gather.9.cloned.1.call-update) | async-done | bytes 2097168 | tf_op jit(solution)/shard_map/all_gather | solution.py:56
  363.8 1.7 fusion.41
  365.4 0.0 copy-start.2
  365.5 0.3 concatenate.28
  365.8 1.1 copy.15
  366.9 0.6 copy.16
  367.5 0.0 copy-done.2
  367.5 0.0 copy-start.1
  367.5 5.8 %fusion.44 = (f32[2,256]{1,0:T(2,128)S(1)}, f32[2,256,2816]{2,1,0:T(8,128)}) fusion(pred[2816]{0:T(1024)(128)(4,1)S(1)} %concatenate.26, bf16[2048,2,128]{2,0,1:T(8,128)(2,1)} %copy.15, bf16[768,2,128]{2,0,1:T(8,128)(2,1)S(1)} %copy.14, f32[256,2,128]{2,0,1:T(8,128)} %copy.13, f32[128]{0:T(128)S(1)} %copy-done.2, f32[256,2]{0,1:T(2,128)S(1)} %add_rsqrt_fusion.1), kind=kOutput, calls=%fused_computation.50 | convolution fusion | flops 377948928 | bytes 7478528 | tf_op jit(solution)/shard_map/sub | solution.py:67
  373.3 0.0 copy-done.1
  373.3 3.8 fusion.20
  377.1 126.6 %all-gather.11.cloned.1.call-done = bf16[256,3072]{0,1:T(8,128)(2,1)} async-done(((bf16[256,48]{0,1:T(8,128)(2,1)}), bf16[256,3072]{0,1:T(8,128)(2,1)}) %all-gather.11.cloned.1.call-update) | async-done | bytes 1572880 | tf_op jit(solution)/shard_map/all_gather | solution.py:73
  503.7 2.0 convolution_convert_fusion
  505.8 1.6 copy.17
  507.4 0.0 reduce-scatter.4.cloned.1.call-update
  507.4 42.5 %reduce-scatter.4.cloned.1.call-done = bf16[384,256]{1,0:T(8,128)(2,1)} async-done(((bf16[3072,256]{1,0:T(8,128)(2,1)}), bf16[384,256]{1,0:T(8,128)(2,1)}) %reduce-scatter.4.cloned.1.call-update) | async-done | bytes 196624
  549.9 1.7 copy.18
  (16 shorter events, 0.2 us)
Async XLA Ops:
  6.5 25.0 %copy-start = (f32[128]{0:T(128)S(1)}, f32[128]{0:T(128)}, u32[]{:S(2)}) copy-start(f32[128]{0:T(128)} %param.12) | copy-start | bytes 1540
  6.5 162.2 %all-gather.5.cloned.1.call-start = ((), (), s32[]{:S(2)}) async-start(), calls=%async_computation.1 | async-start | bytes 4792320 | tf_op jit(solution)/shard_map/all_gather | solution.py:38
  7.3 206.0 %all-gather.7.cloned.1.call-start = ((), (), s32[]{:S(2)}) async-start(), calls=%async_computation.2 | async-start | bytes 1769472 | tf_op jit(solution)/shard_map/all_gather | solution.py:35
  8.0 355.8 %all-gather.9.cloned.1.call-start = ((), (), s32[]{:S(2)}) async-start(), calls=%async_computation.3 | async-start | bytes 2129920 | tf_op jit(solution)/shard_map/all_gather | solution.py:56
  172.3 331.5 %all-gather.11.cloned.1.call-start = ((), (), s32[]{:S(2)}) async-start(), calls=%async_computation.4 | async-start | bytes 1597440 | tf_op jit(solution)/shard_map/all_gather | solution.py:73
  172.9 377.0 %reduce-scatter.4.cloned.1.call-start = ((), (), s32[]{:S(2)}) async-start(), calls=%async_computation.5 | async-start | bytes 1769472
  217.8 10.1 %collective-permute-start = (bf16[2,256,256]{1,2,0:T(8,128)(2,1)S(1)}, bf16[2,256,256]{1,2,0:T(8,128)(2,1)S(1)}, u32[]{:S(2)}, u32[]{:S(2)}) collective-permute-start(bf16[2,256,256]{1,2,0:T(8,128)(2,1)S(1)} %pad_maximum_fusion.1), channel_id=1, source_target_pairs={{0,8},{8,16},{16,24},{24,32},{32,40},{40,48},{48,56},{56,64},{64,7... | collective-permute-start | bytes 786440 | tf_op jit(solution)/shard_map/ppermute | solution.py:17
  224.6 7.8 %collective-permute-start.1 = (bf16[2,256,256]{1,2,0:T(8,128)(2,1)S(1)}, bf16[2,256,256]{1,2,0:T(8,128)(2,1)S(1)}, u32[]{:S(2)}, u32[]{:S(2)}) collective-permute-start(bf16[2,256,256]{1,2,0:T(8,128)(2,1)S(1)} %pad_maximum_fusion.1), channel_id=1, source_target_pairs={{8,0},{16,8},{24,16},{32,24},{40,32},{48,40},{56,48},{64,56},{72,6... | collective-permute-start | bytes 786440 | tf_op jit(solution)/shard_map/ppermute | solution.py:20
  365.4 2.1 copy-start.2
  367.5 5.8 %copy-start.1 = (bf16[1,768,256]{1,2,0:T(8,128)(2,1)S(1)}, bf16[1,768,256]{1,2,0:T(8,128)(2,1)}, u32[]{:S(2)}) copy-start(bf16[1,768,256]{1,2,0:T(8,128)(2,1)} %get-tuple-element.7) | copy-start | bytes 1179652
Sparse Core Ops, SparseCore 0:
  10.4 158.3 all-gather.4
  170.9 42.3 all-gather.6
  216.6 147.1 all-gather.8
  366.9 136.7 all-gather.10
  507.5 42.3 reduce-scatter.3
where the time goes:
time: 561 us; the launch traced here: 558 us
  waiting for transfers between devices  483 us (86%)
  blocking collectives  23.5 us (4%)
  matrix products  18.4 us (3%)
  between operations  14 us (2%)
  local copies, waits for them, and re-layouts  9.16 us (2%)
  starting transfers between devices  8.92 us (2%)
    all_gather x1, waiting for transfers between devices, local(): panel = lax.all_gather(qkv_weight, 'lon', axis=1, tiled=True)  137 us
    all_gather x1, waiting for transfers between devices, local(): style_all = lax.all_gather(style_pair, 'lon', axis=1, tiled=True)  130 us
    all_gather x1, waiting for transfers between devices, local(): lax.all_gather(out_weight, 'lon', axis=1, tiled=True)  127 us
    unnamed x6, waiting for transfers between devices  44.5 us
    all_gather x1, waiting for transfers between devices, local(): lax.all_gather(image_tokens, 'tp', axis=1, tiled=True)  39.7 us
    all_gather x1, blocking collectives, local(): lax.all_gather(style_tokens, 'tp', axis=1, tiled=True)  23.5 us
  transfers between devices with their start and end apart: 7, of which 7 were waited for; matrix products, arithmetic and copies ran while one was open for 4% of the time, Pallas kernels for 0%

commit v1 on v0

v1 whole, which is shorter than its diff:
```python
import math

import jax
import jax.numpy as jnp
from jax import lax
from jax.experimental import pallas as pl
from jax.experimental.pallas import tpu as pltpu
from jax.sharding import Mesh, PartitionSpec as P

HEAD = 128
AXES = ("x_hi", "z", "core", "y", "x_lo")
LON = ("x_hi", "z", "core")
TP = ("y", "x_lo")
F32 = jnp.float32
BF16 = jnp.bfloat16


def spread(block, axes):
    count = lax.axis_size(axes)
    return lax.all_to_all(
        jnp.broadcast_to(block[None], (count,) + block.shape), axes, 0, 0, tiled=True
    )


def unit(values, gain):
    return values * lax.rsqrt(jnp.mean(values * values, axis=-1, keepdims=True) + 1e-06) * gain


def pack_kernel(w_ref, o_ref, out_ref):
    copies = out_ref.shape[0] * HEAD // w_ref.shape[2]
    for c in range(w_ref.shape[2] // HEAD):
        lanes = pl.ds(c * HEAD, HEAD)
        row = jnp.concatenate(
            [w_ref[1, :, lanes], w_ref[2, :, lanes], w_ref[0, :, lanes], o_ref[:, lanes]], axis=1
        )
        for r in range(copies):
            out_ref[r * (w_ref.shape[2] // HEAD) + c] = row


def pack(w, o, copies):
    heads = w.shape[2] // HEAD
    return pl.pallas_call(
        pack_kernel,
        out_shape=jax.ShapeDtypeStruct((copies * heads, w.shape[1], 4 * HEAD), BF16),
        name="pack",
    )(w, o)


def project_kernel(
    x_ref, y_ref, s_ref, w_ref, qg_ref, kg_ref, kvx_ref, kvy_ref, qx_ref, qy_ref, skv_ref, acc, sacc
):
    step = pl.program_id(0)
    pieces, count, width = x_ref.shape
    groups, _, rows, _ = s_ref.shape

    @pl.when(step == 0)
    def _():
        acc[...] = jnp.zeros_like(acc)
        sacc[...] = jnp.zeros_like(sacc)

    w = w_ref[...]
    s = jnp.concatenate([s_ref[:, i].reshape(groups * rows, width) for i in range(pieces)], axis=1)
    sacc[...] += jnp.dot(s, w[:, : 2 * HEAD], preferred_element_type=F32)
    for i, t_ref in enumerate((x_ref, y_ref)):
        t = jnp.concatenate([t_ref[j] for j in range(pieces)], axis=1)
        acc[i] += jnp.dot(t, w, preferred_element_type=F32)

    @pl.when(step == pl.num_programs(0) - 1)
    def _():
        kg, qg = kg_ref[...], qg_ref[...]
        skv_ref[:, :HEAD] = unit(sacc[:, :HEAD], kg).astype(BF16)
        skv_ref[:, HEAD:] = sacc[:, HEAD:].astype(BF16)
        for i, (kv_ref, q_ref) in enumerate(((kvx_ref, qx_ref), (kvy_ref, qy_ref))):
            kv_ref[:, :HEAD] = unit(acc[i, :, :HEAD], kg).astype(BF16)
            kv_ref[:, HEAD:] = acc[i, :, HEAD : 2 * HEAD].astype(BF16)
            q_ref[...] = unit(acc[i, :, 2 * HEAD :], qg).astype(BF16)


def project(x, y, s, w, query_gain, key_gain):
    parts, count, width = x.shape
    groups, _, rows, _ = s.shape
    pieces = 2
    slab = pl.BlockSpec((pieces, count, width), lambda i: (i, 0, 0))
    gain = pl.BlockSpec((1, HEAD), lambda i: (0, 0))

    def out(tokens, wide):
        spec = pl.BlockSpec((tokens, wide * HEAD), lambda i: (0, 0))
        return spec, jax.ShapeDtypeStruct((tokens, wide * HEAD), BF16)

    outs = [out(count, 2), out(count, 2), out(count, 1), out(count, 1), out(groups * rows, 2)]
    return pl.pallas_call(
        project_kernel,
        grid=(parts // pieces,),
        in_specs=[
            slab,
            slab,
            pl.BlockSpec((groups, pieces, rows, width), lambda i: (0, i, 0, 0)),
            pl.BlockSpec((pieces * width, 3 * HEAD), lambda i: (i, 0)),
            gain,
            gain,
        ],
        out_specs=[o[0] for o in outs],
        out_shape=[o[1] for o in outs],
        scratch_shapes=[
            pltpu.VMEM((2, count, 3 * HEAD), F32),
            pltpu.VMEM((groups * rows, 2 * HEAD), F32),
        ],
        compiler_params=pltpu.CompilerParams(vmem_limit_bytes=16 << 20),
        name="project",
    )(x, y, s, w, query_gain, key_gain)


NT = (((1,), (1,)), ((), ()))


def attend_kernel(
    fx_ref, fy_ref, qx_ref, qy_ref, kvx_ref, kvy_ref, hx_ref, hy_ref, s_ref, ox_ref, oy_ref, near, q
):
    i = pl.program_id(0)
    count = kvx_ref.shape[0]

    @pl.when(i == 0)
    def _():
        near[pl.ds(0, count)] = kvx_ref[...]
        near[pl.ds(count, count)] = kvy_ref[...]
        near[pl.ds(2 * count, count)] = hx_ref[...]
        q[...] = qx_ref[...]

    @pl.when(i == 1)
    def _():
        near[pl.ds(2 * count, count)] = hy_ref[...]
        q[...] = qy_ref[...]

    flag = jnp.where(i == 0, fx_ref[0, 0], fy_ref[0, 0])
    scale = 1.0 / math.sqrt(HEAD)
    close = lax.dot_general(q[...], near[:, :HEAD], NT, preferred_element_type=F32) * scale
    far = lax.dot_general(q[...], s_ref[:, :HEAD], NT, preferred_element_type=F32) * scale
    far = jnp.where(flag > 0, far, -1e30)
    peak = jnp.maximum(
        jnp.max(close, axis=-1, keepdims=True), jnp.max(far, axis=-1, keepdims=True)
    )
    close = jnp.exp(close - peak)
    far = jnp.exp(far - peak)
    total = jnp.sum(close, axis=-1, keepdims=True) + jnp.sum(far, axis=-1, keepdims=True)
    share = 1.0 / total
    out = jnp.dot((close * share).astype(BF16), near[:, HEAD:], preferred_element_type=F32)
    out += jnp.dot((far * share).astype(BF16), s_ref[:, HEAD:], preferred_element_type=F32)
    out = out.astype(BF16)

    @pl.when(i == 0)
    def _():
        ox_ref[...] = out

    @pl.when(i == 1)
    def _():
        oy_ref[...] = out


def attend(flags, queries, kvs, halos, style):
    count = queries[0].shape[0]

    def whole(array):
        return pl.BlockSpec(array.shape, lambda i: (0, 0))

    operands = [*queries, *kvs, *halos, style]
    return pl.pallas_call(
        attend_kernel,
        grid=(2,),
        in_specs=[pl.BlockSpec(memory_space=pltpu.SMEM)] * 2 + [whole(a) for a in operands],
        out_specs=[whole(q) for q in queries],
        out_shape=[jax.ShapeDtypeStruct(q.shape, BF16) for q in queries],
        scratch_shapes=[
            pltpu.VMEM((3 * count, 2 * HEAD), BF16),
            pltpu.VMEM((count, HEAD), BF16),
        ],
        compiler_params=pltpu.CompilerParams(vmem_limit_bytes=24 << 20),
        name="attend",
    )(*flags, *operands)


def mix_kernel(ax_ref, ay_ref, wx_ref, wy_ref, o_ref):
    a = jnp.concatenate([ax_ref[...], ay_ref[...]], axis=1)
    w = jnp.concatenate([wx_ref[...], wy_ref[...]], axis=1)
    o_ref[0] = lax.dot_general(a, w, NT, preferred_element_type=F32).astype(BF16)


def mix(attended, panels, columns, parts):
    count = attended[0].shape[0]
    width = panels[0].shape[0] // parts
    rows = pl.BlockSpec((count, HEAD), lambda i: (0, 0))
    return pl.pallas_call(
        mix_kernel,
        grid=(parts,),
        in_specs=[rows, rows]
        + [pl.BlockSpec((width, HEAD), lambda i, c=c: (i, c)) for c in columns],
        out_specs=pl.BlockSpec((1, count, width), lambda i: (i, 0, 0)),
        out_shape=jax.ShapeDtypeStruct((parts, count, width), BF16),
        compiler_params=pltpu.CompilerParams(vmem_limit_bytes=12 << 20),
        name="mix",
    )(*attended, *panels)


def local(image_tokens, style_tokens, qkv_weight, out_weight, query_gain, key_gain, attend_flags):
    parts = lax.axis_size(TP)
    cores = lax.axis_size("core")
    halves = lax.axis_size("x_hi")
    rows = lax.axis_size("z")
    depth = qkv_weight.shape[1]

    def swap(block):
        return lax.ppermute(block, "core", [(0, 1), (1, 0)])

    mine = pack(qkv_weight, out_weight.T, halves)
    plane = lax.all_to_all(mine, ("x_hi", "core"), 0, 0, tiled=True)
    plane = plane.reshape(halves, cores * depth, 4 * HEAD)
    with jax.named_scope("panel"):
        panel = lax.all_gather(plane, "z", axis=1, tiled=True).reshape(-1, 4 * HEAD)

    image_tokens, style_tokens, attend_flags, _ = lax.optimization_barrier(
        (image_tokens, style_tokens, attend_flags, plane)
    )
    with jax.named_scope("image"):
        own = spread(image_tokens, TP)
    other = swap(own)
    with jax.named_scope("style"):
        style = spread(style_tokens, ("x_hi", "core") + TP)
    style = style.reshape((halves * cores, parts) + style_tokens.shape)
    flags = (attend_flags, swap(attend_flags))

    kvx, kvy, qx, qy, style_kv = project(
        own, other, style, panel, query_gain.reshape(1, HEAD), key_gain.reshape(1, HEAD)
    )
    with jax.named_scope("far"):
        far = spread(style_kv, "z").reshape(-1, 2 * HEAD)
    chips = halves * rows
    outward = [
        (c * cores + k, (c + 1 - 2 * k) % chips * cores + k) for c in range(chips) for k in (0, 1)
    ]
    inward = [
        (c * cores + k, (c - 1 + 2 * k) % chips * cores + k) for c in range(chips) for k in (0, 1)
    ]
    halo_x = lax.ppermute(kvy, LON, outward)
    halo_y = lax.ppermute(kvx, LON, inward)
    out_panel = swap(panel[:, 3 * HEAD :])

    ax, ay = attend(flags, (qx, qy), (kvx, kvy), (halo_x, halo_y), far)
    shares = mix((ax, swap(ay)), (panel, out_panel), (3, 0), parts)
    shares = lax.all_to_all(shares, TP, 0, 0, tiled=True)
    return jnp.sum(shares.astype(F32), axis=0).astype(BF16)


def solution(mesh):
    fine = Mesh(mesh.devices.reshape(2, 16, 2, 4, 2), AXES)
    in_specs = (
        P(LON, TP),
        P(LON, TP),
        P(None, LON, TP),
        P(TP, LON),
        P(),
        P(),
        P(LON, None),
    )
    return jax.shard_map(
        local, mesh=fine, in_specs=in_specs, out_specs=P(LON, TP), check_vma=False
    )
```

time: 561 us -> 210 us (0.37)
  waiting for transfers between devices: 483 us -> 37.7 us
  blocking collectives: 23.5 us -> 80.8 us
  starting transfers between devices: 8.92 us -> 47.5 us
  matrix products: 18.4 us -> 0 us
  Pallas kernels: 0 us -> 15.3 us
    all_gather x4 -> x1, waiting for transfers between devices: 434 us -> 18.9 us  [local(): panel = lax.all_gather(plane, 'z', axis=1, tiled=True).reshape(-1, 4 * HEAD)]
    all_to_all x0 -> x4, blocking collectives: none -> 80.8 us  [the longest x2 39.4 us: spread(): lax.all_to_all(jnp.broadcast_to(block[None], (count,) + block.shape), axe...]
    unnamed x6 -> x1, waiting for transfers between devices: 44.5 us -> 0.02 us
    ppermute x2 -> x6, starting transfers between devices: 8.76 us -> 40.6 us  [the longest x4 31.6 us: swap(): return lax.ppermute(block, 'core', [(0, 1), (1, 0)])]
    all_gather x1 -> x0, blocking collectives: 23.5 us -> none  [local(): lax.all_gather(style_tokens, 'tp', axis=1, tiled=True)]
    pallas_call x0 -> x4, Pallas kernels: none -> 15.3 us  [the longest x1 5.42 us: attend(): pl.pallas_call(attend_kernel, grid=(2,), in_specs=[pl.BlockSpec(memory_sp...]
    ppermute x2 -> x6, waiting for transfers between devices: 5 us -> 18.8 us  [the longest x1 16.9 us: local(): halo_x = lax.ppermute(kvy, LON, outward)]
    dot_general x4 -> x0, matrix products: 12.6 us -> none  [the longest x1 4.26 us: local(): jnp.einsum('td,jdc->jtc', image_full, panel, preferred_element_type=jnp.f...]
  transfers between devices with their start and end apart: 7 -> 8, of which waited for: 7 -> 4; matrix products, arithmetic and copies ran while one was open for 4% -> 1% of each run, Pallas kernels for 0% -> 3%
where the time goes in v1:
time: 210 us; the launch traced here: 208 us
  blocking collectives  80.8 us (38%)
  starting transfers between devices  47.5 us (23%)
  waiting for transfers between devices  37.7 us (18%)
  Pallas kernels  15.3 us (7%)
  between operations  14.2 us (7%)
  local copies, waits for them, and re-layouts  12.2 us (6%)
    all_to_all x2, blocking collectives, spread(): lax.all_to_all(jnp.broadcast_to(block[None], (count,) + block.shape), axe...  39.4 us
    ppermute x4, starting transfers between devices, swap(): return lax.ppermute(block, 'core', [(0, 1), (1, 0)])  31.6 us
    all_to_all x1, blocking collectives, local(): shares = lax.all_to_all(shares, TP, 0, 0, tiled=True)  24.5 us
    all_gather x1, waiting for transfers between devices, local(): panel = lax.all_gather(plane, 'z', axis=1, tiled=True).reshape(-1, 4 * HEAD)  18.9 us
    all_to_all x1, blocking collectives, local(): plane = lax.all_to_all(mine, ('x_hi', 'core'), 0, 0, tiled=True)  17 us
    ppermute x1, waiting for transfers between devices, local(): halo_x = lax.ppermute(kvy, LON, outward)  16.9 us
    unnamed x26, local copies, waits for them, and re-layouts  8.94 us
    ppermute x1, starting transfers between devices, local(): halo_x = lax.ppermute(kvy, LON, outward)  7.1 us
  transfers between devices with their start and end apart: 8, of which 4 were waited for; matrix products, arithmetic and copies ran while one was open for 1% of the time, Pallas kernels for 3%

profile of v1, /device:TPU:1, one launch (start us, length us, event | category | flops | bytes accessed | tf_op | source)
XLA Modules:
  0.0 208.5 jit_solution(16709767873278742610)
XLA Ops:
  6.5 0.0 all-gather.2.cloned.1.call-start
  6.5 1.6 pack.1
  8.1 17.0 %all_to_all.25 = bf16[4,48,512]{2,1,0:T(8,128)(2,1)} all-to-all(bf16[4,48,512]{2,1,0:T(8,128)(2,1)} %pack.1), channel_id=1, replica_groups=mesh['x_hi'=2,'z'=16,'core'=2,'y'=4,'x_lo'=2] {'x_hi','core'}, dimensions={0} | all-to-all | bytes 393216 | tf_op jit(solution)/shard_map/all_to_all | solution.py:214
  25.1 0.0 all-gather.2.cloned.1.call-update
  25.1 1.1 broadcast_in_dim.6
  26.2 0.0 copy-start.12
  26.2 23.1 %all_to_all.26.x_ref = bf16[8,256,384]{2,1,0:T(8,128)(2,1)S(1)} all-to-all(bf16[8,256,384]{2,1,0:T(8,128)(2,1)S(1)} %broadcast_in_dim.6), channel_id=1, replica_groups=mesh['x_hi'=2,'z'=16,'core'=2,'y'=4,'x_lo'=2] {'y','x_lo'}, dimensions={0} | all-to-all | bytes 3145728 | tf_op jit(solution)/shard_map/image/all_to_all | solution.py:20
  49.3 0.0 copy-start.10
  49.3 0.0 copy-start.11
  49.3 3.9 %collective-permute-start.1 = (bf16[8,256,384]{2,1,0:T(8,128)(2,1)S(1)}, bf16[8,256,384]{2,1,0:T(8,128)(2,1)S(1)}, u32[]{:S(2)}, u32[]{:S(2)}) collective-permute-start(bf16[8,256,384]{2,1,0:T(8,128)(2,1)S(1)} %all_to_all.26.x_ref), channel_id=1, source_target_pairs={{0,8},{8,0},{1,9},{9,1},{2,10},{10,2},{3,11},{11,3},{4,12},{12,4},... | collective-permute-start | bytes 4718600 | tf_op jit(solution)/shard_map/ppermute | solution.py:211
  53.1 0.0 copy-done.12
  53.2 0.1 broadcast_in_dim.7
  53.2 16.3 %all_to_all.27 = bf16[32,32,384]{2,1,0:T(8,128)(2,1)S(1)} all-to-all(bf16[32,32,384]{2,1,0:T(8,128)(2,1)S(1)} %broadcast_in_dim.7), channel_id=1, replica_groups=mesh['x_hi'=2,'z'=16,'core'=2,'y'=4,'x_lo'=2] {'x_hi','core','y','x_lo'}, dimensions={0} | all-to-all | bytes 1572864 | tf_op jit(solution)/shard_map/style/all_to_all | solution.py:20
  69.5 0.0 collective-permute-done.1.y_ref
  69.5 0.0 copy-start.2
  69.5 1.2 copy-done.2
  70.7 18.9 %all-gather.2.cloned.1.call-done = bf16[2,1536,512]{2,1,0:T(8,128)(2,1)} async-done(((bf16[2,96,512]{2,1,0:T(8,128)(2,1)}), bf16[2,1536,512]{2,1,0:T(8,128)(2,1)}) %all-gather.2.cloned.1.call-update) | async-done | bytes 3145744 | tf_op jit(solution)/shard_map/panel/all_gather | solution.py:217
  89.5 0.0 copy-done.10
  89.5 0.0 copy-done.11
  89.5 1.9 copy-done
  91.4 1.4 copy-done.3
  92.8 3.3 %project.1 = (bf16[256,256]{1,0:T(8,128)(2,1)S(1)}, bf16[256,256]{1,0:T(8,128)(2,1)S(1)}, bf16[256,128]{1,0:T(8,128)(2,1)S(1)}, bf16[256,128]{1,0:T(8,128)(2,1)S(1)}, bf16[128,256]{1,0:T(8,128)(2,1)S(1)}) custom-call(bf16[8,256,384]{2,1,0:T(8,128)(2,1)S(1)} %all_to_all.26.x_ref, bf16[8,256,384]{2,1,0:T(8,128)(2,1)S(1)} %copy-done.3, ...), custom_call_target="tpu_custom_call" | custom-call | tf_op jit(solution)/shard_map/project/pallas_call | solution.py:91
  96.1 0.0 copy-start.6
  96.1 0.6 copy-done.6
  96.7 0.6 copy-done.8
  97.3 1.1 broadcast_in_dim.8
  98.4 6.9 %all-to-all-start.3 = ((bf16[16,128,256]{2,1,0:T(8,128)(2,1)}), bf16[16,128,256]{2,1,0:T(8,128)(2,1)}, u32[]{:S(2)}, u32[]{:S(2)}) async-start(bf16[16,128,256]{2,1,0:T(8,128)(2,1)} %broadcast_in_dim.8), calls=%async_computation.3 | async-start | bytes 2097152 | tf_op jit(solution)/shard_map/far/all_to_all | solution.py:20
  105.3 0.0 copy-done.1
  105.4 1.0 slice.4
  106.3 12.6 %collective-permute-start.5 = (bf16[3072,128]{1,0:T(8,128)(2,1)}, bf16[3072,128]{1,0:T(8,128)(2,1)}, u32[]{:S(2)}, u32[]{:S(2)}) collective-permute-start(bf16[3072,128]{1,0:T(8,128)(2,1)} %slice.4), channel_id=1, source_target_pairs={{0,8},{8,0},{1,9},{9,1},{2,10},{10,2},{3,11},{11,3},{4,12},{12,4},... | collective-permute-start | bytes 2359304 | tf_op jit(solution)/shard_map/ppermute | solution.py:211
  119.0 7.1 %collective-permute-start.2 = (bf16[256,256]{1,0:T(8,128)(2,1)S(1)}, bf16[256,256]{1,0:T(8,128)(2,1)S(1)}, u32[]{:S(2)}, u32[]{:S(2)}) collective-permute-start(bf16[256,256]{1,0:T(8,128)(2,1)S(1)} %get-tuple-element.21.kvy_ref), channel_id=1, source_target_pairs={{0,16},{8,504},{16,32},{24,8},{32,48},{40,24},{48,64},{56,40},{64,... | collective-permute-start | bytes 393224 | tf_op jit(solution)/shard_map/ppermute | solution.py:242
  126.1 1.9 collective-permute-start.3
  128.6 2.4 %collective-permute-start = (s32[1,1]{1,0:T(1,128)}, s32[1,1]{1,0:T(1,128)}, u32[]{:S(2)}, u32[]{:S(2)}) collective-permute-start(s32[1,1]{1,0:T(1,128)} %param.13), channel_id=1, source_target_pairs={{0,8},{8,0},{1,9},{9,1},{2,10},{10,2},{3,11},{11,3},{4,12},{12,4},... | collective-permute-start | bytes 20 | tf_op jit(solution)/shard_map/ppermute | solution.py:211
  131.0 1.1 collective-permute-done.fy_ref
  132.1 16.9 %collective-permute-done.2.hx_ref = bf16[256,256]{1,0:T(8,128)(2,1)S(1)} collective-permute-done((bf16[256,256]{1,0:T(8,128)(2,1)S(1)}, bf16[256,256]{1,0:T(8,128)(2,1)S(1)}, u32[]{:S(2)}, u32[]{:S(2)}) %collective-permute-start.2) | collective-permute-done | bytes 131104 | tf_op jit(solution)/shard_map/ppermute | solution.py:242
  148.9 0.0 collective-permute-done.3.hy_ref
  148.9 0.7 copy-done.4
  149.6 0.0 all-to-all-done.3
  149.6 0.9 copy-done.5
  150.5 0.8 copy-done.7
  151.3 0.8 copy-done.9
  152.2 5.4 %attend.1 = (bf16[256,128]{1,0:T(8,128)(2,1)S(1)}, bf16[256,128]{1,0:T(8,128)(2,1)S(1)}) custom-call(s32[1,1]{1,0:T(1,128)S(6)} %copy.8.fx_ref, s32[1,1]{1,0:T(1,128)} %collective-permute-done.fy_ref, bf16[256,128]{1,0:T(8,128)(2,1)S(1)} %copy-done.7, bf16[256,128]{1,0:T(8,128)(2,1)S(1)} %copy-done.9, bf16[256,256]{1,0:T(8,128)(2,1)S(1)} %get-tuple-element.20.kvx_ref, ...), custom_call_target="tpu_custom_call" | custom-call | tf_op jit(solution)/shard_map/attend/pallas_call | solution.py:166
  157.6 12.7 %collective-permute-start.4 = (bf16[256,128]{1,0:T(8,128)(2,1)S(1)}, bf16[256,128]{1,0:T(8,128)(2,1)S(1)}, u32[]{:S(2)}, u32[]{:S(2)}) collective-permute-start(bf16[256,128]{1,0:T(8,128)(2,1)S(1)} %get-tuple-element.24), channel_id=1, source_target_pairs={{0,8},{8,0},{1,9},{9,1},{2,10},{10,2},{3,11},{11,3},{4,12},{12,4},... | collective-permute-start | bytes 196616 | tf_op jit(solution)/shard_map/ppermute | solution.py:211
  170.3 0.0 collective-permute-done.5.wy_ref
  170.3 0.9 collective-permute-done.4.ay_ref
  171.2 5.0 %mix.1 = bf16[8,256,384]{2,1,0:T(8,128)(2,1)S(1)} custom-call(bf16[256,128]{1,0:T(8,128)(2,1)S(1)} %get-tuple-element.23.ax_ref, bf16[256,128]{1,0:T(8,128)(2,1)S(1)} %collective-permute-done.4.ay_ref, bf16[3072,512]{1,0:T(8,128)(2,1)S(1)} %bitcast.9, bf16[3072,128]{1,0:T(8,128)(2,1)} %collective-permute-done.5.wy_ref), custom_call_target="tpu_custom_call" | custom-call | tf_op jit(solution)/shard_map/mix/pallas_call | solution.py:191
  176.2 24.5 %all_to_all.28 = bf16[8,256,384]{2,1,0:T(8,128)(2,1)S(1)} all-to-all(bf16[8,256,384]{2,1,0:T(8,128)(2,1)S(1)} %mix.1), channel_id=1, replica_groups=mesh['x_hi'=2,'z'=16,'core'=2,'y'=4,'x_lo'=2] {'y','x_lo'}, dimensions={0} | all-to-all | bytes 3145728 | tf_op jit(solution)/shard_map/all_to_all | solution.py:248
  200.7 0.9 reduce_sum.12
  (8 shorter events, 0.0 us)
Async XLA Ops:
  6.5 83.0 %all-gather.2.cloned.1.call-start = ((), (), s32[]{:S(2)}) async-start(), calls=%async_computation.5 | async-start | bytes 3342336 | tf_op jit(solution)/shard_map/panel/all_gather | solution.py:217
  26.2 27.0 %copy-start.12 = (bf16[32,384]{1,0:T(8,128)(2,1)S(1)}, bf16[32,384]{1,0:T(8,128)(2,1)}, u32[]{:S(2)}) copy-start(bf16[32,384]{1,0:T(8,128)(2,1)} %param.8) | copy-start | bytes 73732
  49.3 40.3 %copy-start.10 = (f32[128]{0:T(128)S(1)}, f32[128]{0:T(128)}, u32[]{:S(2)}) copy-start(f32[128]{0:T(128)} %param.11) | copy-start | bytes 1540
  49.3 40.3 %copy-start.11 = (f32[128]{0:T(128)S(1)}, f32[128]{0:T(128)}, u32[]{:S(2)}) copy-start(f32[128]{0:T(128)} %param.12) | copy-start | bytes 1540
  49.3 20.2 %collective-permute-start.1 = (bf16[8,256,384]{2,1,0:T(8,128)(2,1)S(1)}, bf16[8,256,384]{2,1,0:T(8,128)(2,1)S(1)}, u32[]{:S(2)}, u32[]{:S(2)}) collective-permute-start(bf16[8,256,384]{2,1,0:T(8,128)(2,1)S(1)} %all_to_all.26.x_ref), channel_id=1, source_target_pairs={{0,8},{8,0},{1,9},{9,1},{2,10},{10,2},{3,11},{11,3},{4,12},{12,4},... | collective-permute-start | bytes 4718600 | tf_op jit(solution)/shard_map/ppermute | solution.py:211
  69.5 1.2 copy-start.2
  89.5 1.9 copy-start
  91.4 1.4 copy-start.3
  96.1 0.6 copy-start.6
  96.7 0.6 copy-start.8
  97.3 8.0 %copy-start.1 = (bf16[2,1536,512]{2,1,0:T(8,128)(2,1)S(1)}, bf16[2,1536,512]{2,1,0:T(8,128)(2,1)}, u32[]{:S(2)}) copy-start(bf16[2,1536,512]{2,1,0:T(8,128)(2,1)} %all-gather.2.cloned.1.call-done) | copy-start | bytes 9437188
  98.4 51.2 %all-to-all-start.3 = ((bf16[16,128,256]{2,1,0:T(8,128)(2,1)}), bf16[16,128,256]{2,1,0:T(8,128)(2,1)}, u32[]{:S(2)}, u32[]{:S(2)}) async-start(bf16[16,128,256]{2,1,0:T(8,128)(2,1)} %broadcast_in_dim.8), calls=%async_computation.3 | async-start | bytes 2097152 | tf_op jit(solution)/shard_map/far/all_to_all | solution.py:20
  106.3 64.0 %collective-permute-start.5 = (bf16[3072,128]{1,0:T(8,128)(2,1)}, bf16[3072,128]{1,0:T(8,128)(2,1)}, u32[]{:S(2)}, u32[]{:S(2)}) collective-permute-start(bf16[3072,128]{1,0:T(8,128)(2,1)} %slice.4), channel_id=1, source_target_pairs={{0,8},{8,0},{1,9},{9,1},{2,10},{10,2},{3,11},{11,3},{4,12},{12,4},... | collective-permute-start | bytes 2359304 | tf_op jit(solution)/shard_map/ppermute | solution.py:211
  119.0 30.0 %collective-permute-start.2 = (bf16[256,256]{1,0:T(8,128)(2,1)S(1)}, bf16[256,256]{1,0:T(8,128)(2,1)S(1)}, u32[]{:S(2)}, u32[]{:S(2)}) collective-permute-start(bf16[256,256]{1,0:T(8,128)(2,1)S(1)} %get-tuple-element.21.kvy_ref), channel_id=1, source_target_pairs={{0,16},{8,504},{16,32},{24,8},{32,48},{40,24},{48,64},{56,40},{64,... | collective-permute-start | bytes 393224 | tf_op jit(solution)/shard_map/ppermute | solution.py:242
  126.1 22.9 %collective-permute-start.3 = (bf16[256,256]{1,0:T(8,128)(2,1)S(1)}, bf16[256,256]{1,0:T(8,128)(2,1)S(1)}, u32[]{:S(2)}, u32[]{:S(2)}) collective-permute-start(bf16[256,256]{1,0:T(8,128)(2,1)S(1)} %get-tuple-element.20.kvx_ref), channel_id=1, source_target_pairs={{0,496},{8,24},{16,0},{24,40},{32,16},{40,56},{48,32},{56,72},{64,... | collective-permute-start | bytes 393224 | tf_op jit(solution)/shard_map/ppermute | solution.py:243
  128.6 3.4 %collective-permute-start = (s32[1,1]{1,0:T(1,128)}, s32[1,1]{1,0:T(1,128)}, u32[]{:S(2)}, u32[]{:S(2)}) collective-permute-start(s32[1,1]{1,0:T(1,128)} %param.13), channel_id=1, source_target_pairs={{0,8},{8,0},{1,9},{9,1},{2,10},{10,2},{3,11},{11,3},{4,12},{12,4},... | collective-permute-start | bytes 20 | tf_op jit(solution)/shard_map/ppermute | solution.py:211
  148.9 0.7 copy-start.4
  149.6 0.9 copy-start.5
  150.5 0.8 copy-start.7
  151.3 0.8 copy-start.9
  157.6 13.6 %collective-permute-start.4 = (bf16[256,128]{1,0:T(8,128)(2,1)S(1)}, bf16[256,128]{1,0:T(8,128)(2,1)S(1)}, u32[]{:S(2)}, u32[]{:S(2)}) collective-permute-start(bf16[256,128]{1,0:T(8,128)(2,1)S(1)} %get-tuple-element.24), channel_id=1, source_target_pairs={{0,8},{8,0},{1,9},{9,1},{2,10},{10,2},{3,11},{11,3},{4,12},{12,4},... | collective-permute-start | bytes 196616 | tf_op jit(solution)/shard_map/ppermute | solution.py:211
Sparse Core Ops, SparseCore 0:
  25.2 64.2 all-gather.1

commit v2 on v1

v2 whole, which is shorter than its diff:
```python
import functools
import math

import jax
import jax.numpy as jnp
from jax import lax
from jax.experimental import pallas as pl
from jax.experimental.pallas import tpu as pltpu
from jax.sharding import Mesh, PartitionSpec as P


HEAD = 128
AXES = ("x_hi", "z_hi", "z_lo", "core", "y", "x_lo")
Z = ("z_hi", "z_lo")
LON = ("x_hi",) + Z + ("core",)
TP = ("y", "x_lo")
F32 = jnp.float32
BF16 = jnp.bfloat16


def spread(block, axes):
    count = lax.axis_size(axes)
    return lax.all_to_all(
        jnp.broadcast_to(block[None], (count,) + block.shape), axes, 0, 0, tiled=True
    )


def unit(values, gain):
    return values * lax.rsqrt(jnp.mean(values * values, axis=-1, keepdims=True) + 1e-06) * gain


def pack_kernel(w_ref, o_ref, out_ref):
    copies = out_ref.shape[0] * HEAD // w_ref.shape[2]
    for c in range(w_ref.shape[2] // HEAD):
        lanes = pl.ds(c * HEAD, HEAD)
        row = jnp.concatenate(
            [w_ref[1, :, lanes], w_ref[2, :, lanes], w_ref[0, :, lanes], o_ref[:, lanes]], axis=1
        )
        for r in range(copies):
            out_ref[r * (w_ref.shape[2] // HEAD) + c] = row


def pack(w, o, copies):
    heads = w.shape[2] // HEAD
    return pl.pallas_call(
        pack_kernel,
        out_shape=jax.ShapeDtypeStruct((copies * heads, w.shape[1], 4 * HEAD), BF16),
        name="pack",
    )(w, o)


def project_kernel(
    me_ref,
    x_ref,
    y_ref,
    sx_ref,
    sy_ref,
    w_ref,
    qg_ref,
    kg_ref,
    forward_ref,
    backward_ref,
    low_ref,
    high_ref,
    q_ref,
    acc,
    sacc,
    weights,
    arrived,
):
    step = pl.program_id(0)
    pieces, count, width = x_ref.shape
    groups, _, rows, _ = sx_ref.shape

    def fetch(i):
        lines = pl.ds(i * pieces * width, pieces * width)
        return pltpu.make_async_copy(
            w_ref.at[lines, pl.ds(0, 3 * HEAD)], weights.at[i], arrived.at[i]
        )

    @pl.when(step == 0)
    def _():
        for i in range(weights.shape[0]):
            fetch(i).start()
        acc[...] = jnp.zeros_like(acc)
        sacc[...] = jnp.zeros_like(sacc)

    fetch(step).wait()
    w = weights[step]
    for i, s_ref in enumerate((sx_ref, sy_ref)):
        for g in range(groups):
            s = jnp.concatenate([s_ref[g, j] for j in range(pieces)], axis=1)
            sacc[pl.ds((i * groups + g) * rows, rows)] += jnp.dot(
                s, w[:, : 2 * HEAD], preferred_element_type=F32
            )
    for i, t_ref in enumerate((x_ref, y_ref)):
        t = jnp.concatenate([t_ref[j] for j in range(pieces)], axis=1)
        acc[i] += jnp.dot(t, w, preferred_element_type=F32)

    @pl.when(step == pl.num_programs(0) - 1)
    def _():
        kg, qg = kg_ref[...], qg_ref[...]
        far = 2 * groups * rows
        for half, part_ref in enumerate((low_ref, high_ref)):
            lines = pl.ds(half * far // 2, far // 2)
            k = unit(sacc[lines, :HEAD], kg).astype(BF16)
            v = sacc[lines, HEAD:].astype(BF16)
            for out_ref in (forward_ref, backward_ref):
                out_ref[lines, :HEAD] = k
                out_ref[lines, HEAD:] = v
            part_ref[:, :HEAD] = k
            part_ref[:, HEAD:] = v
        me = me_ref[0]
        lines = pl.ds(far, count)
        for slab, out_ref in enumerate((backward_ref, forward_ref)):
            mine = acc[slab ^ me]
            out_ref[lines, :HEAD] = unit(mine[:, :HEAD], kg).astype(BF16)
            out_ref[lines, HEAD:] = mine[:, HEAD : 2 * HEAD].astype(BF16)
            q_ref[slab] = unit(mine[:, 2 * HEAD :], qg).astype(BF16)


def project(me, slabs, styles, w, query_gain, key_gain):
    parts, count, width = slabs[0].shape
    groups, _, rows, _ = styles[0].shape
    pieces = 2
    far = 2 * groups * rows
    slab = pl.BlockSpec((pieces, count, width), lambda i: (i, 0, 0))
    style = pl.BlockSpec((groups, pieces, rows, width), lambda i: (0, i, 0, 0))
    gain = pl.BlockSpec((1, HEAD), lambda i: (0, 0))

    def out(*shape):
        spec = pl.BlockSpec(shape, lambda i: (0,) * len(shape))
        return spec, jax.ShapeDtypeStruct(shape, BF16)

    pair = (far + count, 2 * HEAD)
    part = (far // 2, 2 * HEAD)
    outs = [out(*pair), out(*pair), out(*part), out(*part), out(2, count, HEAD)]
    return pl.pallas_call(
        project_kernel,
        grid=(parts // pieces,),
        in_specs=[
            pl.BlockSpec(memory_space=pltpu.SMEM),
            slab,
            slab,
            style,
            style,
            pl.BlockSpec(memory_space=pltpu.HBM),
            gain,
            gain,
        ],
        out_specs=[o[0] for o in outs],
        out_shape=[o[1] for o in outs],
        scratch_shapes=[
            pltpu.VMEM((2, count, 3 * HEAD), F32),
            pltpu.VMEM((far, 2 * HEAD), F32),
            pltpu.VMEM((parts // pieces, pieces * width, 3 * HEAD), BF16),
            pltpu.SemaphoreType.DMA((parts // pieces,)),
        ],
        compiler_params=pltpu.CompilerParams(vmem_limit_bytes=58 << 20),
        name="project",
    )(me, *slabs, *styles, w, query_gain, key_gain)


NT = (((1,), (1,)), ((), ()))


def attend_kernel(
    me_ref,
    fx_ref,
    fy_ref,
    q_ref,
    forward_ref,
    backward_ref,
    before_ref,
    after_ref,
    low_ref,
    high_ref,
    ox_ref,
    oy_ref,
    near,
):
    i = pl.program_id(0)
    me = me_ref[0]
    count = q_ref.shape[1]
    style = forward_ref.shape[0] - count
    slab = pl.ds(style, count)

    @pl.when(i == 0)
    def _():
        near[pl.ds(0, count)] = backward_ref[slab]
        near[pl.ds(count, count)] = forward_ref[slab]
        near[pl.ds(2 * count, count)] = before_ref[slab]

    @pl.when(i == 1)
    def _():
        near[pl.ds(2 * count, count)] = after_ref[slab]

    flag = jnp.where(i == me, fx_ref[0, 0], fy_ref[0, 0])
    scale = 1.0 / math.sqrt(HEAD)
    q = q_ref[0]
    lines = pl.ds(0, style)
    refs = [near, *(r.at[lines] for r in (forward_ref, before_ref, after_ref)), low_ref, high_ref]
    scores = []
    for n, ref in enumerate(refs):
        part = lax.dot_general(q, ref[:, :HEAD], NT, preferred_element_type=F32) * scale
        scores.append(jnp.where(flag > 0, part, -1e30) if n else part)
    peak = functools.reduce(jnp.maximum, [jnp.max(s, axis=-1, keepdims=True) for s in scores])
    expo = [jnp.exp(s - peak) for s in scores]
    share = 1.0 / sum(jnp.sum(e, axis=-1, keepdims=True) for e in expo)
    out = sum(
        jnp.dot((e * share).astype(BF16), ref[:, HEAD:], preferred_element_type=F32)
        for e, ref in zip(expo, refs)
    ).astype(BF16)

    @pl.when(i == me)
    def _():
        ox_ref[...] = out

    @pl.when(i != me)
    def _():
        oy_ref[...] = out


def attend(me, flags, query, *keys):
    slabs, count, _ = query.shape
    scalar = pl.BlockSpec(memory_space=pltpu.SMEM)
    out = pl.BlockSpec((count, HEAD), lambda i: (0, 0))
    return pl.pallas_call(
        attend_kernel,
        grid=(slabs,),
        in_specs=[scalar] * 3
        + [pl.BlockSpec((1, count, HEAD), lambda i: (i, 0, 0))]
        + [pl.BlockSpec(k.shape, lambda i: (0, 0)) for k in keys],
        out_specs=[out, out],
        out_shape=[jax.ShapeDtypeStruct((count, HEAD), BF16)] * 2,
        scratch_shapes=[pltpu.VMEM((3 * count, 2 * HEAD), BF16)],
        compiler_params=pltpu.CompilerParams(vmem_limit_bytes=24 << 20),
        name="attend",
    )(me, *flags, query, *keys)


def mix_kernel(ax_ref, ay_ref, wx_ref, wy_ref, o_ref):
    parts, _, width = o_ref.shape
    a = jnp.concatenate([ax_ref[...], ay_ref[...]], axis=1)
    for i in range(parts):
        lines = pl.ds(i * width, width)
        w = jnp.concatenate([wx_ref[lines], wy_ref[lines]], axis=1)
        o_ref[i] = lax.dot_general(a, w, NT, preferred_element_type=F32).astype(BF16)


def mix(attended, panels, parts):
    count = attended[0].shape[0]
    width = panels[0].shape[0] // parts
    return pl.pallas_call(
        mix_kernel,
        out_shape=jax.ShapeDtypeStruct((parts, count, width), BF16),
        compiler_params=pltpu.CompilerParams(vmem_limit_bytes=12 << 20),
        name="mix",
    )(*attended, *panels)


def local(image_tokens, style_tokens, qkv_weight, out_weight, query_gain, key_gain, attend_flags):
    parts = lax.axis_size(TP)
    cores = lax.axis_size("core")
    halves = lax.axis_size("x_hi")
    rows = lax.axis_size(Z)
    depth = qkv_weight.shape[1]

    def swap(block):
        return lax.ppermute(block, "core", [(0, 1), (1, 0)])

    me = lax.axis_index("core").reshape(1)
    mine = pack(qkv_weight, out_weight.T, halves)
    plane = lax.all_to_all(mine, ("x_hi", "core"), 0, 0, tiled=True)
    plane = plane.reshape(halves, cores * depth, 4 * HEAD)
    panel = lax.all_gather(plane, Z, axis=1, tiled=True).reshape(-1, 4 * HEAD)

    image_tokens, style_tokens, attend_flags, _ = lax.optimization_barrier(
        (image_tokens, style_tokens, attend_flags, plane)
    )
    own = spread(image_tokens, TP)
    slabs = (own, swap(own))
    style = spread(style_tokens, "z_hi").reshape(-1, style_tokens.shape[1])
    style = spread(style, ("x_hi",) + TP)
    style = style.reshape((halves, parts) + style.shape[1:])
    styles = (style, swap(style))
    flags = (attend_flags, swap(attend_flags))
    slabs, styles, flags = lax.optimization_barrier((slabs, styles, flags))

    forward, backward, low, high, query = project(
        me, slabs, styles, panel, query_gain.reshape(1, HEAD), key_gain.reshape(1, HEAD)
    )
    chips = halves * rows

    def shift(block, axes, count, by):
        return lax.ppermute(block, axes, [(i, (i + by) % count) for i in range(count)])

    before = shift(forward, ("x_hi",) + Z, chips, 1)
    after = shift(backward, ("x_hi",) + Z, chips, -1)
    low = shift(low, Z, rows, 2)
    high = shift(high, Z, rows, -2)
    panel, query = lax.optimization_barrier((panel, query))
    out_own = panel[:, 3 * HEAD :]
    out_other = swap(out_own)

    ax, ay = attend(me, flags, query, forward, backward, before, after, low, high)
    shares = mix((ax, swap(ay)), (out_own, out_other), parts)
    shares = lax.all_to_all(shares, TP, 0, 0, tiled=True)
    return jnp.sum(shares.astype(F32), axis=0).astype(BF16)


def solution(mesh):
    fine = Mesh(mesh.devices.reshape(2, 4, 4, 2, 4, 2), AXES)
    in_specs = (
        P(LON, TP),
        P(LON, TP),
        P(None, LON, TP),
        P(TP, LON),
        P(),
        P(),
        P(LON, None),
    )
    return jax.shard_map(
        local, mesh=fine, in_specs=in_specs, out_specs=P(LON, TP), check_vma=False
    )
```

time: 210 us -> 183 us (0.87)
  waiting for transfers between devices: 37.7 us -> 20.4 us
  local copies, waits for them, and re-layouts: 12.2 us -> 4.62 us
  starting transfers between devices: 47.5 us -> 40.8 us
  blocking collectives: 80.8 us -> 86.7 us
    all_gather x1, waiting for transfers between devices: 18.9 us -> 0.01 us  [local(): panel = lax.all_gather(plane, Z, axis=1, tiled=True).reshape(-1, 4 * HEAD)]
    all_to_all x1, waiting for transfers between devices: 0.01 us -> 12.7 us  [spread(): lax.all_to_all(jnp.broadcast_to(block[None], (count,) + block.shape), axe...]
    ppermute x2 -> x4, waiting for transfers between devices: 16.9 us -> 5.56 us  [shift(): lax.ppermute(block, axes, [(i, (i + by) % count) for i in range(count)])]
    ppermute x4 -> x5, starting transfers between devices: 31.6 us -> 20.8 us  [swap(): return lax.ppermute(block, 'core', [(0, 1), (1, 0)])]
    unnamed x26 -> x14, local copies, waits for them, and re-layouts: 8.94 us -> 0.03 us
    ppermute x2 -> x4, starting transfers between devices: 9.02 us -> 16.3 us  [shift(): lax.ppermute(block, axes, [(i, (i + by) % count) for i in range(count)])]
    all_to_all x2, blocking collectives: 39.4 us -> 45.1 us  [spread(): lax.all_to_all(jnp.broadcast_to(block[None], (count,) + block.shape), axe...]
    all_to_all x1, starting transfers between devices: 6.91 us -> 3.71 us  [spread(): lax.all_to_all(jnp.broadcast_to(block[None], (count,) + block.shape), axe...]
  transfers between devices with their start and end apart: 8 -> 11, of which waited for: 4 -> 5; matrix products, arithmetic and copies ran while one was open for 1% -> 2% of each run, Pallas kernels for 3% -> 2%
where the time goes in v2:
time: 183 us; the launch traced here: 182 us
  blocking collectives  86.7 us (47%)
  starting transfers between devices  40.8 us (22%)
  waiting for transfers between devices  20.4 us (11%)
  between operations  14.3 us (8%)
  Pallas kernels  14.1 us (8%)
  local copies, waits for them, and re-layouts  4.62 us (3%)
    all_to_all x2, blocking collectives, spread(): lax.all_to_all(jnp.broadcast_to(block[None], (count,) + block.shape), axe...  45.1 us
    all_to_all x1, blocking collectives, local(): shares = lax.all_to_all(shares, TP, 0, 0, tiled=True)  24.7 us
    ppermute x5, starting transfers between devices, swap(): return lax.ppermute(block, 'core', [(0, 1), (1, 0)])  20.8 us
    all_to_all x1, blocking collectives, local(): plane = lax.all_to_all(mine, ('x_hi', 'core'), 0, 0, tiled=True)  16.9 us
    ppermute x4, starting transfers between devices, shift(): lax.ppermute(block, axes, [(i, (i + by) % count) for i in range(count)])  16.3 us
    all_to_all x1, waiting for transfers between devices, spread(): lax.all_to_all(jnp.broadcast_to(block[None], (count,) + block.shape), axe...  12.7 us
    pallas_call x1, Pallas kernels, project(): pl.pallas_call(project_kernel, grid=(parts // pieces,), in_specs=[pl.Bloc...  7.82 us
    ppermute x4, waiting for transfers between devices, shift(): lax.ppermute(block, axes, [(i, (i + by) % count) for i in range(count)])  5.56 us
  transfers between devices with their start and end apart: 11, of which 5 were waited for; matrix products, arithmetic and copies ran while one was open for 2% of the time, Pallas kernels for 2%

profile of v2, /device:TPU:1, one launch (start us, length us, event | category | flops | bytes accessed | tf_op | source)
XLA Modules:
  0.0 181.8 jit_solution(11503851560161271845)
XLA Ops:
  6.5 0.0 all-gather.2.cloned.1.call-start
  6.5 1.6 pack.1
  8.1 16.9 %all_to_all.25 = bf16[4,48,512]{2,1,0:T(8,128)(2,1)} all-to-all(bf16[4,48,512]{2,1,0:T(8,128)(2,1)} %pack.1), channel_id=1, replica_groups=mesh['x_hi'=2,'z_hi'=4,'z_lo'=4,'core'=2,'y'=4,'x_lo'=2] {'x_hi','core'}, dimensions={0} | all-to-all | bytes 393216 | tf_op jit(solution)/shard_map/all_to_all | solution.py:274
  25.1 0.0 all-gather.2.cloned.1.call-update
  25.1 0.7 broadcast_in_dim.9
  25.8 22.2 %all_to_all.26 = bf16[4,32,384]{2,1,0:T(8,128)(2,1)S(1)} all-to-all(bf16[4,32,384]{2,1,0:T(8,128)(2,1)S(1)} %broadcast_in_dim.9), channel_id=1, replica_groups=mesh['x_hi'=2,'z_hi'=4,'z_lo'=4,'core'=2,'y'=4,'x_lo'=2] {'z_hi'}, dimensions={0} | all-to-all | bytes 196608 | tf_op jit(solution)/shard_map/all_to_all | solution.py:23
  48.1 1.1 broadcast_in_dim.8
  49.2 22.8 %all_to_all.27.x_ref = bf16[8,256,384]{2,1,0:T(8,128)(2,1)S(1)} all-to-all(bf16[8,256,384]{2,1,0:T(8,128)(2,1)S(1)} %broadcast_in_dim.8), channel_id=1, replica_groups=mesh['x_hi'=2,'z_hi'=4,'z_lo'=4,'core'=2,'y'=4,'x_lo'=2] {'y','x_lo'}, dimensions={0} | all-to-all | bytes 3145728 | tf_op jit(solution)/shard_map/all_to_all | solution.py:23
  72.0 1.5 broadcast_in_dim.22
  73.5 3.7 %all-to-all-start.3 = ((bf16[16,128,384]{2,1,0:T(8,128)(2,1)}), bf16[16,128,384]{2,1,0:T(8,128)(2,1)S(1)}, u32[]{:S(2)}, u32[]{:S(2)}) async-start(bf16[16,128,384]{2,1,0:T(8,128)(2,1)} %broadcast_in_dim.22), calls=%async_computation.3 | async-start | bytes 3145728 | tf_op jit(solution)/shard_map/all_to_all | solution.py:23
  77.2 0.0 copy-done.3
  77.2 5.9 %collective-permute-start = (bf16[8,256,384]{2,1,0:T(8,128)(2,1)S(1)}, bf16[8,256,384]{2,1,0:T(8,128)(2,1)}, u32[]{:S(2)}, u32[]{:S(2)}) collective-permute-start(bf16[8,256,384]{2,1,0:T(8,128)(2,1)S(1)} %all_to_all.27.x_ref), channel_id=1, source_target_pairs={{0,8},{8,0},{1,9},{9,1},{2,10},{10,2},{3,11},{11,3},{4,12},{12,4},... | collective-permute-start | bytes 4718600 | tf_op jit(solution)/shard_map/ppermute | solution.py:270
  83.1 12.7 %all-to-all-done.3 = bf16[16,128,384]{2,1,0:T(8,128)(2,1)S(1)} async-done(((bf16[16,128,384]{2,1,0:T(8,128)(2,1)}), bf16[16,128,384]{2,1,0:T(8,128)(2,1)S(1)}, u32[]{:S(2)}, u32[]{:S(2)}) %all-to-all-start.3) | async-done | bytes 1572896 | tf_op jit(solution)/shard_map/all_to_all | solution.py:23
  95.8 7.5 %collective-permute-start.1 = (bf16[2,8,128,384]{3,2,1,0:T(8,128)(2,1)S(1)}, bf16[2,8,128,384]{3,2,1,0:T(8,128)(2,1)}, u32[]{:S(2)}, u32[]{:S(2)}) collective-permute-start(bf16[2,8,128,384]{3,2,1,0:T(8,128)(2,1)S(1)} %bitcast.8), channel_id=1, source_target_pairs={{0,8},{8,0},{1,9},{9,1},{2,10},{10,2},{3,11},{11,3},{4,12},{12,4},... | collective-permute-start | bytes 4718600 | tf_op jit(solution)/shard_map/ppermute | solution.py:270
  103.3 1.9 %collective-permute-start.2 = (s32[1,1]{1,0:T(1,128)}, s32[1,1]{1,0:T(1,128)}, u32[]{:S(2)}, u32[]{:S(2)}) collective-permute-start(s32[1,1]{1,0:T(1,128)} %param.13), channel_id=1, source_target_pairs={{0,8},{8,0},{1,9},{9,1},{2,10},{10,2},{3,11},{11,3},{4,12},{12,4},... | collective-permute-start | bytes 20 | tf_op jit(solution)/shard_map/ppermute | solution.py:270
  105.2 1.2 collective-permute-done.2.fy_ref
  106.5 0.0 collective-permute-done.y_ref
  106.5 0.0 collective-permute-done.1.sy_ref
  106.5 0.0 all-gather.2.cloned.1.call-done
  106.5 0.0 copy-done.4
  106.5 7.8 %project.1 = (bf16[768,256]{1,0:T(8,128)(2,1)}, bf16[768,256]{1,0:T(8,128)(2,1)}, bf16[256,256]{1,0:T(8,128)(2,1)}, bf16[256,256]{1,0:T(8,128)(2,1)}, bf16[2,256,128]{2,1,0:T(8,128)(2,1)}) custom-call(s32[1]{0:T(128)} %bitcast.me_ref, bf16[8,256,384]{2,1,0:T(8,128)(2,1)} %copy-done.3, bf16[8,256,384]{2,1,0:T(8,128)(2,1)} %collective-permute-done.y_ref, ...), custom_call_target="tpu_custom_call" | custom-call | tf_op jit(solution)/shard_map/project/pallas_call | solution.py:138
  114.3 0.0 copy-start
  114.3 0.0 copy-start.1
  114.4 0.0 copy-start.6
  114.4 0.0 copy-start.5
  114.4 0.0 copy-start.2
  114.4 1.3 slice.3.wx_ref
  115.7 2.3 %collective-permute-start.8 = (bf16[3072,128]{1,0:T(8,128)(2,1)S(1)}, bf16[3072,128]{1,0:T(8,128)(2,1)S(1)}, u32[]{:S(2)}, u32[]{:S(2)}) collective-permute-start(bf16[3072,128]{1,0:T(8,128)(2,1)S(1)} %slice.3.wx_ref), channel_id=1, source_target_pairs={{0,8},{8,0},{1,9},{9,1},{2,10},{10,2},{3,11},{11,3},{4,12},{12,4},... | collective-permute-start | bytes 2359304 | tf_op jit(solution)/shard_map/ppermute | solution.py:270
  117.9 0.0 copy-done
  117.9 1.9 %collective-permute-start.3 = (bf16[768,256]{1,0:T(8,128)(2,1)S(1)}, bf16[768,256]{1,0:T(8,128)(2,1)S(1)}, u32[]{:S(2)}, u32[]{:S(2)}) collective-permute-start(bf16[768,256]{1,0:T(8,128)(2,1)S(1)} %copy-done), channel_id=1, source_target_pairs={{0,16},{16,32},{32,48},{48,64},{64,80},{80,96},{96,112},{112,128},... | collective-permute-start | bytes 1179656 | tf_op jit(solution)/shard_map/ppermute | solution.py:296
  119.9 0.0 copy-done.1
  119.9 7.0 %collective-permute-start.4 = (bf16[768,256]{1,0:T(8,128)(2,1)S(1)}, bf16[768,256]{1,0:T(8,128)(2,1)S(1)}, u32[]{:S(2)}, u32[]{:S(2)}) collective-permute-start(bf16[768,256]{1,0:T(8,128)(2,1)S(1)} %copy-done.1), channel_id=1, source_target_pairs={{0,496},{16,0},{32,16},{48,32},{64,48},{80,64},{96,80},{112,96},{1... | collective-permute-start | bytes 1179656 | tf_op jit(solution)/shard_map/ppermute | solution.py:296
  126.9 0.0 copy-done.6
  126.9 1.9 %collective-permute-start.5 = (bf16[256,256]{1,0:T(8,128)(2,1)S(1)}, bf16[256,256]{1,0:T(8,128)(2,1)S(1)}, u32[]{:S(2)}, u32[]{:S(2)}) collective-permute-start(bf16[256,256]{1,0:T(8,128)(2,1)S(1)} %copy-done.6), channel_id=1, source_target_pairs={{0,32},{16,48},{32,64},{48,80},{64,96},{80,112},{96,128},{112,144}... | collective-permute-start | bytes 393224 | tf_op jit(solution)/shard_map/ppermute | solution.py:296
  128.8 0.0 copy-done.5
  128.8 5.5 %collective-permute-start.6 = (bf16[256,256]{1,0:T(8,128)(2,1)S(1)}, bf16[256,256]{1,0:T(8,128)(2,1)S(1)}, u32[]{:S(2)}, u32[]{:S(2)}) collective-permute-start(bf16[256,256]{1,0:T(8,128)(2,1)S(1)} %copy-done.5), channel_id=1, source_target_pairs={{0,224},{16,240},{32,0},{48,16},{64,32},{80,48},{96,64},{112,80},{... | collective-permute-start | bytes 393224 | tf_op jit(solution)/shard_map/ppermute | solution.py:296
  134.9 1.4 collective-permute-done.5.low_ref
  136.4 4.1 %collective-permute-done.6.high_ref = bf16[256,256]{1,0:T(8,128)(2,1)S(1)} collective-permute-done((bf16[256,256]{1,0:T(8,128)(2,1)S(1)}, bf16[256,256]{1,0:T(8,128)(2,1)S(1)}, u32[]{:S(2)}, u32[]{:S(2)}) %collective-permute-start.6) | collective-permute-done | bytes 131104 | tf_op jit(solution)/shard_map/ppermute | solution.py:296
  140.5 0.0 collective-permute-done.3.before_ref
  140.5 0.0 collective-permute-done.4.after_ref
  140.5 0.0 copy-done.2
  140.5 4.0 %attend.1 = (bf16[256,128]{1,0:T(8,128)(2,1)S(1)}, bf16[256,128]{1,0:T(8,128)(2,1)S(1)}) custom-call(s32[1]{0:T(128)} %bitcast.me_ref, s32[1,1]{1,0:T(1,128)S(6)} %copy.8.fx_ref, s32[1,1]{1,0:T(1,128)} %collective-permute-done.2.fy_ref, bf16[2,256,128]{2,1,0:T(8,128)(2,1)S(1)} %copy-done.2, bf16[768,256]{1,0:T(8,128)(2,1)S(1)} %copy-done, ...), custom_call_target="tpu_custom_call" | custom-call | tf_op jit(solution)/shard_map/attend/pallas_call | solution.py:228
  144.5 3.2 %collective-permute-start.7 = (bf16[256,128]{1,0:T(8,128)(2,1)S(1)}, bf16[256,128]{1,0:T(8,128)(2,1)S(1)}, u32[]{:S(2)}, u32[]{:S(2)}) collective-permute-start(bf16[256,128]{1,0:T(8,128)(2,1)S(1)} %get-tuple-element.39), channel_id=1, source_target_pairs={{0,8},{8,0},{1,9},{9,1},{2,10},{10,2},{3,11},{11,3},{4,12},{12,4},... | collective-permute-start | bytes 196616 | tf_op jit(solution)/shard_map/ppermute | solution.py:270
  147.8 0.9 collective-permute-done.7.ay_ref
  148.6 0.0 collective-permute-done.8.wy_ref
  148.6 0.7 mix.1
  149.4 24.7 %all_to_all.28 = bf16[8,256,384]{2,1,0:T(8,128)(2,1)S(1)} all-to-all(bf16[8,256,384]{2,1,0:T(8,128)(2,1)S(1)} %mix.1), channel_id=1, replica_groups=mesh['x_hi'=2,'z_hi'=4,'z_lo'=4,'core'=2,'y'=4,'x_lo'=2] {'y','x_lo'}, dimensions={0} | all-to-all | bytes 3145728 | tf_op jit(solution)/shard_map/all_to_all | solution.py:308
  174.0 0.9 reduce_sum.12
  (2 shorter events, 0.0 us)
Async XLA Ops:
  6.5 100.0 %all-gather.2.cloned.1.call-start = ((), (), s32[]{:S(2)}) async-start(), calls=%async_computation.5 | async-start | bytes 3342336 | tf_op jit(solution)/shard_map/all_gather | solution.py:276
  72.0 5.2 %copy-start.3 = (bf16[8,256,384]{2,1,0:T(8,128)(2,1)}, bf16[8,256,384]{2,1,0:T(8,128)(2,1)S(1)}, u32[]{:S(2)}) copy-start(bf16[8,256,384]{2,1,0:T(8,128)(2,1)S(1)} %all_to_all.27.x_ref) | copy-start | bytes 4718596
  73.5 22.3 %all-to-all-start.3 = ((bf16[16,128,384]{2,1,0:T(8,128)(2,1)}), bf16[16,128,384]{2,1,0:T(8,128)(2,1)S(1)}, u32[]{:S(2)}, u32[]{:S(2)}) async-start(bf16[16,128,384]{2,1,0:T(8,128)(2,1)} %broadcast_in_dim.22), calls=%async_computation.3 | async-start | bytes 3145728 | tf_op jit(solution)/shard_map/all_to_all | solution.py:23
  77.2 29.2 %collective-permute-start = (bf16[8,256,384]{2,1,0:T(8,128)(2,1)S(1)}, bf16[8,256,384]{2,1,0:T(8,128)(2,1)}, u32[]{:S(2)}, u32[]{:S(2)}) collective-permute-start(bf16[8,256,384]{2,1,0:T(8,128)(2,1)S(1)} %all_to_all.27.x_ref), channel_id=1, source_target_pairs={{0,8},{8,0},{1,9},{9,1},{2,10},{10,2},{3,11},{11,3},{4,12},{12,4},... | collective-permute-start | bytes 4718600 | tf_op jit(solution)/shard_map/ppermute | solution.py:270
  95.8 10.7 %copy-start.4 = (bf16[16,128,384]{2,1,0:T(8,128)(2,1)}, bf16[16,128,384]{2,1,0:T(8,128)(2,1)S(1)}, u32[]{:S(2)}) copy-start(bf16[16,128,384]{2,1,0:T(8,128)(2,1)S(1)} %all-to-all-done.3) | copy-start | bytes 4718596
  95.8 10.7 %collective-permute-start.1 = (bf16[2,8,128,384]{3,2,1,0:T(8,128)(2,1)S(1)}, bf16[2,8,128,384]{3,2,1,0:T(8,128)(2,1)}, u32[]{:S(2)}, u32[]{:S(2)}) collective-permute-start(bf16[2,8,128,384]{3,2,1,0:T(8,128)(2,1)S(1)} %bitcast.8), channel_id=1, source_target_pairs={{0,8},{8,0},{1,9},{9,1},{2,10},{10,2},{3,11},{11,3},{4,12},{12,4},... | collective-permute-start | bytes 4718600 | tf_op jit(solution)/shard_map/ppermute | solution.py:270
  103.3 3.2 %collective-permute-start.2 = (s32[1,1]{1,0:T(1,128)}, s32[1,1]{1,0:T(1,128)}, u32[]{:S(2)}, u32[]{:S(2)}) collective-permute-start(s32[1,1]{1,0:T(1,128)} %param.13), channel_id=1, source_target_pairs={{0,8},{8,0},{1,9},{9,1},{2,10},{10,2},{3,11},{11,3},{4,12},{12,4},... | collective-permute-start | bytes 20 | tf_op jit(solution)/shard_map/ppermute | solution.py:270
  114.3 3.6 %copy-start = (bf16[768,256]{1,0:T(8,128)(2,1)S(1)}, bf16[768,256]{1,0:T(8,128)(2,1)}, u32[]{:S(2)}) copy-start(bf16[768,256]{1,0:T(8,128)(2,1)} %get-tuple-element.34.forward_ref) | copy-start | bytes 1179652
  114.3 5.5 %copy-start.1 = (bf16[768,256]{1,0:T(8,128)(2,1)S(1)}, bf16[768,256]{1,0:T(8,128)(2,1)}, u32[]{:S(2)}) copy-start(bf16[768,256]{1,0:T(8,128)(2,1)} %get-tuple-element.35.backward_ref) | copy-start | bytes 1179652
  114.4 12.5 %copy-start.6 = (bf16[256,256]{1,0:T(8,128)(2,1)S(1)}, bf16[256,256]{1,0:T(8,128)(2,1)}, u32[]{:S(2)}) copy-start(bf16[256,256]{1,0:T(8,128)(2,1)} %get-tuple-element.36) | copy-start | bytes 393220
  114.4 14.4 %copy-start.5 = (bf16[256,256]{1,0:T(8,128)(2,1)S(1)}, bf16[256,256]{1,0:T(8,128)(2,1)}, u32[]{:S(2)}) copy-start(bf16[256,256]{1,0:T(8,128)(2,1)} %get-tuple-element.37) | copy-start | bytes 393220
  114.4 26.1 %copy-start.2 = (bf16[2,256,128]{2,1,0:T(8,128)(2,1)S(1)}, bf16[2,256,128]{2,1,0:T(8,128)(2,1)}, u32[]{:S(2)}) copy-start(bf16[2,256,128]{2,1,0:T(8,128)(2,1)} %get-tuple-element.33.q_ref) | copy-start | bytes 393220
  115.7 33.0 %collective-permute-start.8 = (bf16[3072,128]{1,0:T(8,128)(2,1)S(1)}, bf16[3072,128]{1,0:T(8,128)(2,1)S(1)}, u32[]{:S(2)}, u32[]{:S(2)}) collective-permute-start(bf16[3072,128]{1,0:T(8,128)(2,1)S(1)} %slice.3.wx_ref), channel_id=1, source_target_pairs={{0,8},{8,0},{1,9},{9,1},{2,10},{10,2},{3,11},{11,3},{4,12},{12,4},... | collective-permute-start | bytes 2359304 | tf_op jit(solution)/shard_map/ppermute | solution.py:270
  117.9 22.6 %collective-permute-start.3 = (bf16[768,256]{1,0:T(8,128)(2,1)S(1)}, bf16[768,256]{1,0:T(8,128)(2,1)S(1)}, u32[]{:S(2)}, u32[]{:S(2)}) collective-permute-start(bf16[768,256]{1,0:T(8,128)(2,1)S(1)} %copy-done), channel_id=1, source_target_pairs={{0,16},{16,32},{32,48},{48,64},{64,80},{80,96},{96,112},{112,128},... | collective-permute-start | bytes 1179656 | tf_op jit(solution)/shard_map/ppermute | solution.py:296
  119.9 20.6 %collective-permute-start.4 = (bf16[768,256]{1,0:T(8,128)(2,1)S(1)}, bf16[768,256]{1,0:T(8,128)(2,1)S(1)}, u32[]{:S(2)}, u32[]{:S(2)}) collective-permute-start(bf16[768,256]{1,0:T(8,128)(2,1)S(1)} %copy-done.1), channel_id=1, source_target_pairs={{0,496},{16,0},{32,16},{48,32},{64,48},{80,64},{96,80},{112,96},{1... | collective-permute-start | bytes 1179656 | tf_op jit(solution)/shard_map/ppermute | solution.py:296
  126.9 9.5 %collective-permute-start.5 = (bf16[256,256]{1,0:T(8,128)(2,1)S(1)}, bf16[256,256]{1,0:T(8,128)(2,1)S(1)}, u32[]{:S(2)}, u32[]{:S(2)}) collective-permute-start(bf16[256,256]{1,0:T(8,128)(2,1)S(1)} %copy-done.6), channel_id=1, source_target_pairs={{0,32},{16,48},{32,64},{48,80},{64,96},{80,112},{96,128},{112,144}... | collective-permute-start | bytes 393224 | tf_op jit(solution)/shard_map/ppermute | solution.py:296
  128.8 11.7 %collective-permute-start.6 = (bf16[256,256]{1,0:T(8,128)(2,1)S(1)}, bf16[256,256]{1,0:T(8,128)(2,1)S(1)}, u32[]{:S(2)}, u32[]{:S(2)}) collective-permute-start(bf16[256,256]{1,0:T(8,128)(2,1)S(1)} %copy-done.5), channel_id=1, source_target_pairs={{0,224},{16,240},{32,0},{48,16},{64,32},{80,48},{96,64},{112,80},{... | collective-permute-start | bytes 393224 | tf_op jit(solution)/shard_map/ppermute | solution.py:296
  144.5 4.1 %collective-permute-start.7 = (bf16[256,128]{1,0:T(8,128)(2,1)S(1)}, bf16[256,128]{1,0:T(8,128)(2,1)S(1)}, u32[]{:S(2)}, u32[]{:S(2)}) collective-permute-start(bf16[256,128]{1,0:T(8,128)(2,1)S(1)} %get-tuple-element.39), channel_id=1, source_target_pairs={{0,8},{8,0},{1,9},{9,1},{2,10},{10,2},{3,11},{11,3},{4,12},{12,4},... | collective-permute-start | bytes 196616 | tf_op jit(solution)/shard_map/ppermute | solution.py:270
Sparse Core Ops, SparseCore 0:
  25.2 65.6 all-gather.1

commit v3 on v2

--- a/solution.py
+++ b/solution.py
@@ -64,7 +64,7 @@
     high_ref,
     q_ref,
     acc,
-    sacc,
+    qacc,
     weights,
     arrived,
 ):
@@ -83,19 +83,17 @@
         for i in range(weights.shape[0]):
             fetch(i).start()
         acc[...] = jnp.zeros_like(acc)
-        sacc[...] = jnp.zeros_like(sacc)
+        qacc[...] = jnp.zeros_like(qacc)
 
     fetch(step).wait()
     w = weights[step]
-    for i, s_ref in enumerate((sx_ref, sy_ref)):
-        for g in range(groups):
-            s = jnp.concatenate([s_ref[g, j] for j in range(pieces)], axis=1)
-            sacc[pl.ds((i * groups + g) * rows, rows)] += jnp.dot(
-                s, w[:, : 2 * HEAD], preferred_element_type=F32
-            )
-    for i, t_ref in enumerate((x_ref, y_ref)):
-        t = jnp.concatenate([t_ref[j] for j in range(pieces)], axis=1)
-        acc[i] += jnp.dot(t, w, preferred_element_type=F32)
+    tokens = [(t_ref, ()) for t_ref in (x_ref, y_ref)]
+    tokens += [(s_ref, (g,)) for s_ref in (sx_ref, sy_ref) for g in range(groups)]
+    t = jnp.concatenate(
+        [jnp.concatenate([r[i + (j,)] for j in range(pieces)], axis=1) for r, i in tokens], axis=0
+    )
+    acc[...] += jnp.dot(t, w[:, : 2 * HEAD], preferred_element_type=F32)
+    qacc[...] += jnp.dot(t[: 2 * count], w[:, 2 * HEAD :], preferred_element_type=F32)
 
     @pl.when(step == pl.num_programs(0) - 1)
     def _():
@@ -103,8 +101,9 @@
         far = 2 * groups * rows
         for half, part_ref in enumerate((low_ref, high_ref)):
             lines = pl.ds(half * far // 2, far // 2)
-            k = unit(sacc[lines, :HEAD], kg).astype(BF16)
-            v = sacc[lines, HEAD:].astype(BF16)
+            source = pl.ds(2 * count + half * far // 2, far // 2)
+            k = unit(acc[source, :HEAD], kg).astype(BF16)
+            v = acc[source, HEAD:].astype(BF16)
             for out_ref in (forward_ref, backward_ref):
                 out_ref[lines, :HEAD] = k
                 out_ref[lines, HEAD:] = v
@@ -113,10 +112,10 @@
         me = me_ref[0]
         lines = pl.ds(far, count)
         for slab, out_ref in enumerate((backward_ref, forward_ref)):
-            mine = acc[slab ^ me]
-            out_ref[lines, :HEAD] = unit(mine[:, :HEAD], kg).astype(BF16)
-            out_ref[lines, HEAD:] = mine[:, HEAD : 2 * HEAD].astype(BF16)
-            q_ref[slab] = unit(mine[:, 2 * HEAD :], qg).astype(BF16)
+            mine = pl.ds(pl.multiple_of((slab ^ me) * count, count), count)
+            out_ref[lines, :HEAD] = unit(acc[mine, :HEAD], kg).astype(BF16)
+            out_ref[lines, HEAD:] = acc[mine, HEAD:].astype(BF16)
+            q_ref[slab] = unit(qacc[mine], qg).astype(BF16)
 
 
 def project(me, slabs, styles, w, query_gain, key_gain):
@@ -151,8 +150,8 @@
         out_specs=[o[0] for o in outs],
         out_shape=[o[1] for o in outs],
         scratch_shapes=[
-            pltpu.VMEM((2, count, 3 * HEAD), F32),
-            pltpu.VMEM((far, 2 * HEAD), F32),
+            pltpu.VMEM((2 * count + far, 2 * HEAD), F32),
+            pltpu.VMEM((2 * count, HEAD), F32),
             pltpu.VMEM((parts // pieces, pieces * width, 3 * HEAD), BF16),
             pltpu.SemaphoreType.DMA((parts // pieces,)),
         ],
@@ -278,9 +277,16 @@
     image_tokens, style_tokens, attend_flags, _ = lax.optimization_barrier(
         (image_tokens, style_tokens, attend_flags, plane)
     )
+
+    def shift(block, axes, count, by):
+        return lax.ppermute(block, axes, [(i, (i + by) % count) for i in range(count)])
+
+    step = rows // 4
+    style = [style_tokens]
+    style += [shift(style_tokens, Z, rows, i * step) for i in (1, 2, 3)]
+    style = jnp.concatenate(style, axis=0)
     own = spread(image_tokens, TP)
     slabs = (own, swap(own))
-    style = spread(style_tokens, "z_hi").reshape(-1, style_tokens.shape[1])
     style = spread(style, ("x_hi",) + TP)
     style = style.reshape((halves, parts) + style.shape[1:])
     styles = (style, swap(style))
@@ -291,10 +297,6 @@
         me, slabs, styles, panel, query_gain.reshape(1, HEAD), key_gain.reshape(1, HEAD)
     )
     chips = halves * rows
-
-    def shift(block, axes, count, by):
-        return lax.ppermute(block, axes, [(i, (i + by) % count) for i in range(count)])
-
     before = shift(forward, ("x_hi",) + Z, chips, 1)
     after = shift(backward, ("x_hi",) + Z, chips, -1)
     low = shift(low, Z, rows, 2)

time: 183 us -> 178 us (0.973)
  blocking collectives: 86.7 us -> 42 us
  starting transfers between devices: 40.8 us -> 72.9 us
  waiting for transfers between devices: 20.4 us -> 27.2 us
    all_to_all x2 -> x0, blocking collectives: 45.1 us -> none  [spread(): lax.all_to_all(jnp.broadcast_to(block[None], (count,) + block.shape), axe...]
    ppermute x4 -> x7, starting transfers between devices: 16.3 us -> 37.1 us  [shift(): lax.ppermute(block, axes, [(i, (i + by) % count) for i in range(count)])]
    ppermute x5, starting transfers between devices: 20.8 us -> 27.2 us  [swap(): return lax.ppermute(block, 'core', [(0, 1), (1, 0)])]
    all_to_all x1 -> x2, starting transfers between devices: 3.71 us -> 8.59 us  [spread(): lax.all_to_all(jnp.broadcast_to(block[None], (count,) + block.shape), axe...]
    ppermute x4 -> x7, waiting for transfers between devices: 5.56 us -> 9.97 us  [shift(): lax.ppermute(block, axes, [(i, (i + by) % count) for i in range(count)])]
    all_to_all x1 -> x2, waiting for transfers between devices: 12.7 us -> 14.1 us  [spread(): lax.all_to_all(jnp.broadcast_to(block[None], (count,) + block.shape), axe...]
    broadcast_in_dim x3 -> x2, local copies, waits for them, and re-layouts: 3.31 us -> 3.74 us  [spread(): jnp.broadcast_to(block[None], (count,) + block.shape)]
  transfers between devices with their start and end apart: 11 -> 15, of which waited for: 5 -> 7; matrix products, arithmetic and copies ran while one was open for 2% -> 2% of each run, Pallas kernels for 2% -> 2%
where the time goes in v3:
time: 178 us; the launch traced here: 177 us
  starting transfers between devices  72.9 us (41%)
  blocking collectives  42 us (24%)
  waiting for transfers between devices  27.2 us (15%)
  between operations  14.3 us (8%)
  Pallas kernels  14 us (8%)
  local copies, waits for them, and re-layouts  5.05 us (3%)
    ppermute x7, starting transfers between devices, shift(): lax.ppermute(block, axes, [(i, (i + by) % count) for i in range(count)])  37.1 us
    ppermute x5, starting transfers between devices, swap(): return lax.ppermute(block, 'core', [(0, 1), (1, 0)])  27.2 us
    all_to_all x1, blocking collectives, local(): shares = lax.all_to_all(shares, TP, 0, 0, tiled=True)  25.1 us
    all_to_all x1, blocking collectives, local(): plane = lax.all_to_all(mine, ('x_hi', 'core'), 0, 0, tiled=True)  17 us
    all_to_all x2, waiting for transfers between devices, spread(): lax.all_to_all(jnp.broadcast_to(block[None], (count,) + block.shape), axe...  14.1 us
    ppermute x7, waiting for transfers between devices, shift(): lax.ppermute(block, axes, [(i, (i + by) % count) for i in range(count)])  9.97 us
    all_to_all x2, starting transfers between devices, spread(): lax.all_to_all(jnp.broadcast_to(block[None], (count,) + block.shape), axe...  8.59 us
    pallas_call x1, Pallas kernels, project(): pl.pallas_call(project_kernel, grid=(parts // pieces,), in_specs=[pl.Bloc...  7.78 us
  transfers between devices with their start and end apart: 15, of which 7 were waited for; matrix products, arithmetic and copies ran while one was open for 2% of the time, Pallas kernels for 2%

profile of v3, /device:TPU:1, one launch (start us, length us, event | category | flops | bytes accessed | tf_op | source)
XLA Modules:
  0.0 176.5 jit_solution(1877750582758265295)
XLA Ops:
  6.5 0.0 all-gather.2.cloned.1.call-start
  6.5 1.6 pack.1
  8.1 17.0 %all_to_all.20 = bf16[4,48,512]{2,1,0:T(8,128)(2,1)} all-to-all(bf16[4,48,512]{2,1,0:T(8,128)(2,1)} %pack.1), channel_id=1, replica_groups=mesh['x_hi'=2,'z_hi'=4,'z_lo'=4,'core'=2,'y'=4,'x_lo'=2] {'x_hi','core'}, dimensions={0} | all-to-all | bytes 393216 | tf_op jit(solution)/shard_map/all_to_all | solution.py:273
  25.1 0.0 all-gather.2.cloned.1.call-update
  25.1 2.2 %broadcast_in_dim.4 = bf16[8,256,384]{2,1,0:T(8,128)(2,1)} broadcast(bf16[256,384]{1,0:T(8,128)(2,1)} %param.7), dimensions={1,2} | broadcast | bytes 1769472 | tf_op jit(solution)/shard_map/broadcast_in_dim | solution.py:24
  27.3 3.7 %all-to-all-start.1 = ((bf16[8,256,384]{2,1,0:T(8,128)(2,1)}), bf16[8,256,384]{2,1,0:T(8,128)(2,1)S(1)}, u32[]{:S(2)}, u32[]{:S(2)}) async-start(bf16[8,256,384]{2,1,0:T(8,128)(2,1)} %broadcast_in_dim.4), calls=%async_computation.1 | async-start | bytes 3145728 | tf_op jit(solution)/shard_map/all_to_all | solution.py:23
  31.1 0.0 copy-done.5
  31.1 5.0 %collective-permute-start.1 = (bf16[32,384]{1,0:T(8,128)(2,1)S(1)}, bf16[32,384]{1,0:T(8,128)(2,1)S(1)}, u32[]{:S(2)}, u32[]{:S(2)}) collective-permute-start(bf16[32,384]{1,0:T(8,128)(2,1)S(1)} %copy-done.5), channel_id=1, source_target_pairs={{0,64},{16,80},{32,96},{48,112},{64,128},{80,144},{96,160},{112,17... | collective-permute-start | bytes 73736 | tf_op jit(solution)/shard_map/ppermute | solution.py:282
  36.1 10.6 %collective-permute-start.2 = (bf16[32,384]{1,0:T(8,128)(2,1)S(1)}, bf16[32,384]{1,0:T(8,128)(2,1)S(1)}, u32[]{:S(2)}, u32[]{:S(2)}) collective-permute-start(bf16[32,384]{1,0:T(8,128)(2,1)S(1)} %copy-done.5), channel_id=1, source_target_pairs={{0,128},{16,144},{32,160},{48,176},{64,192},{80,208},{96,224},{112... | collective-permute-start | bytes 73736 | tf_op jit(solution)/shard_map/ppermute | solution.py:282
  46.7 5.2 %collective-permute-start.3 = (bf16[32,384]{1,0:T(8,128)(2,1)S(1)}, bf16[32,384]{1,0:T(8,128)(2,1)S(1)}, u32[]{:S(2)}, u32[]{:S(2)}) collective-permute-start(bf16[32,384]{1,0:T(8,128)(2,1)S(1)} %copy-done.5), channel_id=1, source_target_pairs={{0,192},{16,208},{32,224},{48,240},{64,0},{80,16},{96,32},{112,48}... | collective-permute-start | bytes 73736 | tf_op jit(solution)/shard_map/ppermute | solution.py:282
  51.9 0.0 collective-permute-done.1
  51.9 0.0 collective-permute-done.2
  51.9 4.3 %collective-permute-done.3 = bf16[32,384]{1,0:T(8,128)(2,1)S(1)} collective-permute-done((bf16[32,384]{1,0:T(8,128)(2,1)S(1)}, bf16[32,384]{1,0:T(8,128)(2,1)S(1)}, u32[]{:S(2)}, u32[]{:S(2)}) %collective-permute-start.3) | collective-permute-done | bytes 24608 | tf_op jit(solution)/shard_map/ppermute | solution.py:282
  56.2 0.0 all-to-all-done.1.x_ref
  56.2 0.0 copy-start.3
  56.2 1.5 broadcast_in_dim.5
  57.7 4.9 %all-to-all-start.2 = ((bf16[16,128,384]{2,1,0:T(8,128)(2,1)}), bf16[16,128,384]{2,1,0:T(8,128)(2,1)S(1)}, u32[]{:S(2)}, u32[]{:S(2)}) async-start(bf16[16,128,384]{2,1,0:T(8,128)(2,1)} %broadcast_in_dim.5), calls=%async_computation.2 | async-start | bytes 3145728 | tf_op jit(solution)/shard_map/all_to_all | solution.py:23
  62.6 5.3 %collective-permute-start = (bf16[8,256,384]{2,1,0:T(8,128)(2,1)S(1)}, bf16[8,256,384]{2,1,0:T(8,128)(2,1)}, u32[]{:S(2)}, u32[]{:S(2)}) collective-permute-start(bf16[8,256,384]{2,1,0:T(8,128)(2,1)S(1)} %all-to-all-done.1.x_ref), channel_id=1, source_target_pairs={{0,8},{8,0},{1,9},{9,1},{2,10},{10,2},{3,11},{11,3},{4,12},{12,4},... | collective-permute-start | bytes 4718600 | tf_op jit(solution)/shard_map/ppermute | solution.py:269
  67.9 14.1 %all-to-all-done.2 = bf16[16,128,384]{2,1,0:T(8,128)(2,1)S(1)} async-done(((bf16[16,128,384]{2,1,0:T(8,128)(2,1)}), bf16[16,128,384]{2,1,0:T(8,128)(2,1)S(1)}, u32[]{:S(2)}, u32[]{:S(2)}) %all-to-all-start.2) | async-done | bytes 1572896 | tf_op jit(solution)/shard_map/all_to_all | solution.py:23
  82.0 6.5 %collective-permute-start.4 = (bf16[2,8,128,384]{3,2,1,0:T(8,128)(2,1)S(1)}, bf16[2,8,128,384]{3,2,1,0:T(8,128)(2,1)}, u32[]{:S(2)}, u32[]{:S(2)}) collective-permute-start(bf16[2,8,128,384]{3,2,1,0:T(8,128)(2,1)S(1)} %bitcast.7), channel_id=1, source_target_pairs={{0,8},{8,0},{1,9},{9,1},{2,10},{10,2},{3,11},{11,3},{4,12},{12,4},... | collective-permute-start | bytes 4718600 | tf_op jit(solution)/shard_map/ppermute | solution.py:269
  88.5 1.9 %collective-permute-start.5 = (s32[1,1]{1,0:T(1,128)}, s32[1,1]{1,0:T(1,128)}, u32[]{:S(2)}, u32[]{:S(2)}) collective-permute-start(s32[1,1]{1,0:T(1,128)} %param.13), channel_id=1, source_target_pairs={{0,8},{8,0},{1,9},{9,1},{2,10},{10,2},{3,11},{11,3},{4,12},{12,4},... | collective-permute-start | bytes 20 | tf_op jit(solution)/shard_map/ppermute | solution.py:269
  90.5 1.4 collective-permute-done.5.fy_ref
  91.8 0.0 collective-permute-done.y_ref
  91.8 0.0 collective-permute-done.4.sy_ref
  91.8 0.9 all-gather.2.cloned.1.call-done
  92.7 7.8 %project.1 = (bf16[768,256]{1,0:T(8,128)(2,1)}, bf16[768,256]{1,0:T(8,128)(2,1)}, bf16[256,256]{1,0:T(8,128)(2,1)}, bf16[256,256]{1,0:T(8,128)(2,1)}, bf16[2,256,128]{2,1,0:T(8,128)(2,1)}) custom-call(s32[1]{0:T(128)} %bitcast.me_ref, bf16[8,256,384]{2,1,0:T(8,128)(2,1)} %copy-done.3, bf16[8,256,384]{2,1,0:T(8,128)(2,1)} %collective-permute-done.y_ref, ...), custom_call_target="tpu_custom_call" | custom-call | tf_op jit(solution)/shard_map/project/pallas_call | solution.py:137
  100.6 0.0 copy-start.7
  100.6 0.0 copy-start.6
  100.6 0.0 copy-start.2
  100.6 1.3 slice.3.wx_ref
  101.9 10.4 %collective-permute-start.11 = (bf16[3072,128]{1,0:T(8,128)(2,1)S(1)}, bf16[3072,128]{1,0:T(8,128)(2,1)S(1)}, u32[]{:S(2)}, u32[]{:S(2)}) collective-permute-start(bf16[3072,128]{1,0:T(8,128)(2,1)S(1)} %slice.3.wx_ref), channel_id=1, source_target_pairs={{0,8},{8,0},{1,9},{9,1},{2,10},{10,2},{3,11},{11,3},{4,12},{12,4},... | collective-permute-start | bytes 2359304 | tf_op jit(solution)/shard_map/ppermute | solution.py:269
  112.3 2.6 %collective-permute-start.6 = (bf16[768,256]{1,0:T(8,128)(2,1)S(1)}, bf16[768,256]{1,0:T(8,128)(2,1)S(1)}, u32[]{:S(2)}, u32[]{:S(2)}) collective-permute-start(bf16[768,256]{1,0:T(8,128)(2,1)S(1)} %copy-done), channel_id=1, source_target_pairs={{0,16},{16,32},{32,48},{48,64},{64,80},{80,96},{96,112},{112,128},... | collective-permute-start | bytes 1179656 | tf_op jit(solution)/shard_map/ppermute | solution.py:282
  114.9 0.0 copy-done.1
  115.0 6.3 %collective-permute-start.7 = (bf16[768,256]{1,0:T(8,128)(2,1)S(1)}, bf16[768,256]{1,0:T(8,128)(2,1)S(1)}, u32[]{:S(2)}, u32[]{:S(2)}) collective-permute-start(bf16[768,256]{1,0:T(8,128)(2,1)S(1)} %copy-done.1), channel_id=1, source_target_pairs={{0,496},{16,0},{32,16},{48,32},{64,48},{80,64},{96,80},{112,96},{1... | collective-permute-start | bytes 1179656 | tf_op jit(solution)/shard_map/ppermute | solution.py:282
  121.2 1.9 %collective-permute-start.8 = (bf16[256,256]{1,0:T(8,128)(2,1)S(1)}, bf16[256,256]{1,0:T(8,128)(2,1)S(1)}, u32[]{:S(2)}, u32[]{:S(2)}) collective-permute-start(bf16[256,256]{1,0:T(8,128)(2,1)S(1)} %copy-done.7), channel_id=1, source_target_pairs={{0,32},{16,48},{32,64},{48,80},{64,96},{80,112},{96,128},{112,144}... | collective-permute-start | bytes 393224 | tf_op jit(solution)/shard_map/ppermute | solution.py:282
  123.2 0.0 copy-done.6
  123.2 5.5 %collective-permute-start.9 = (bf16[256,256]{1,0:T(8,128)(2,1)S(1)}, bf16[256,256]{1,0:T(8,128)(2,1)S(1)}, u32[]{:S(2)}, u32[]{:S(2)}) collective-permute-start(bf16[256,256]{1,0:T(8,128)(2,1)S(1)} %copy-done.6), channel_id=1, source_target_pairs={{0,224},{16,240},{32,0},{48,16},{64,32},{80,48},{96,64},{112,80},{... | collective-permute-start | bytes 393224 | tf_op jit(solution)/shard_map/ppermute | solution.py:282
  129.3 1.2 collective-permute-done.8.low_ref
  130.5 4.5 %collective-permute-done.9.high_ref = bf16[256,256]{1,0:T(8,128)(2,1)S(1)} collective-permute-done((bf16[256,256]{1,0:T(8,128)(2,1)S(1)}, bf16[256,256]{1,0:T(8,128)(2,1)S(1)}, u32[]{:S(2)}, u32[]{:S(2)}) %collective-permute-start.9) | collective-permute-done | bytes 131104 | tf_op jit(solution)/shard_map/ppermute | solution.py:282
  135.0 0.0 collective-permute-done.6.before_ref
  135.0 0.0 collective-permute-done.7.after_ref
  135.0 4.0 %attend.1 = (bf16[256,128]{1,0:T(8,128)(2,1)S(1)}, bf16[256,128]{1,0:T(8,128)(2,1)S(1)}) custom-call(s32[1]{0:T(128)} %bitcast.me_ref, s32[1,1]{1,0:T(1,128)S(6)} %copy.8.fx_ref, s32[1,1]{1,0:T(1,128)} %collective-permute-done.5.fy_ref, bf16[2,256,128]{2,1,0:T(8,128)(2,1)S(1)} %copy-done.2, bf16[768,256]{1,0:T(8,128)(2,1)S(1)} %copy-done, ...), custom_call_target="tpu_custom_call" | custom-call | tf_op jit(solution)/shard_map/attend/pallas_call | solution.py:227
  139.0 3.1 %collective-permute-start.10 = (bf16[256,128]{1,0:T(8,128)(2,1)S(1)}, bf16[256,128]{1,0:T(8,128)(2,1)S(1)}, u32[]{:S(2)}, u32[]{:S(2)}) collective-permute-start(bf16[256,128]{1,0:T(8,128)(2,1)S(1)} %get-tuple-element.39), channel_id=1, source_target_pairs={{0,8},{8,0},{1,9},{9,1},{2,10},{10,2},{3,11},{11,3},{4,12},{12,4},... | collective-permute-start | bytes 196616 | tf_op jit(solution)/shard_map/ppermute | solution.py:269
  142.0 0.9 collective-permute-done.10.ay_ref
  142.9 0.0 collective-permute-done.11.wy_ref
  142.9 0.7 mix.1
  143.6 25.1 %all_to_all.21 = bf16[8,256,384]{2,1,0:T(8,128)(2,1)S(1)} all-to-all(bf16[8,256,384]{2,1,0:T(8,128)(2,1)S(1)} %mix.1), channel_id=1, replica_groups=mesh['x_hi'=2,'z_hi'=4,'z_lo'=4,'core'=2,'y'=4,'x_lo'=2] {'y','x_lo'}, dimensions={0} | all-to-all | bytes 3145728 | tf_op jit(solution)/shard_map/all_to_all | solution.py:310
  168.7 0.9 reduce_sum.12
  (10 shorter events, 0.0 us)
Async XLA Ops:
  6.5 86.2 %all-gather.2.cloned.1.call-start = ((), (), s32[]{:S(2)}) async-start(), calls=%async_computation.4 | async-start | bytes 3342336 | tf_op jit(solution)/shard_map/all_gather | solution.py:275
  27.3 3.7 %copy-start.5 = (bf16[32,384]{1,0:T(8,128)(2,1)S(1)}, bf16[32,384]{1,0:T(8,128)(2,1)}, u32[]{:S(2)}) copy-start(bf16[32,384]{1,0:T(8,128)(2,1)} %param.8) | copy-start | bytes 73732
  27.3 28.9 %all-to-all-start.1 = ((bf16[8,256,384]{2,1,0:T(8,128)(2,1)}), bf16[8,256,384]{2,1,0:T(8,128)(2,1)S(1)}, u32[]{:S(2)}, u32[]{:S(2)}) async-start(bf16[8,256,384]{2,1,0:T(8,128)(2,1)} %broadcast_in_dim.4), calls=%async_computation.1 | async-start | bytes 3145728 | tf_op jit(solution)/shard_map/all_to_all | solution.py:23
  31.1 20.8 %collective-permute-start.1 = (bf16[32,384]{1,0:T(8,128)(2,1)S(1)}, bf16[32,384]{1,0:T(8,128)(2,1)S(1)}, u32[]{:S(2)}, u32[]{:S(2)}) collective-permute-start(bf16[32,384]{1,0:T(8,128)(2,1)S(1)} %copy-done.5), channel_id=1, source_target_pairs={{0,64},{16,80},{32,96},{48,112},{64,128},{80,144},{96,160},{112,17... | collective-permute-start | bytes 73736 | tf_op jit(solution)/shard_map/ppermute | solution.py:282
  36.1 15.8 %collective-permute-start.2 = (bf16[32,384]{1,0:T(8,128)(2,1)S(1)}, bf16[32,384]{1,0:T(8,128)(2,1)S(1)}, u32[]{:S(2)}, u32[]{:S(2)}) collective-permute-start(bf16[32,384]{1,0:T(8,128)(2,1)S(1)} %copy-done.5), channel_id=1, source_target_pairs={{0,128},{16,144},{32,160},{48,176},{64,192},{80,208},{96,224},{112... | collective-permute-start | bytes 73736 | tf_op jit(solution)/shard_map/ppermute | solution.py:282
  46.7 9.5 %collective-permute-start.3 = (bf16[32,384]{1,0:T(8,128)(2,1)S(1)}, bf16[32,384]{1,0:T(8,128)(2,1)S(1)}, u32[]{:S(2)}, u32[]{:S(2)}) collective-permute-start(bf16[32,384]{1,0:T(8,128)(2,1)S(1)} %copy-done.5), channel_id=1, source_target_pairs={{0,192},{16,208},{32,224},{48,240},{64,0},{80,16},{96,32},{112,48}... | collective-permute-start | bytes 73736 | tf_op jit(solution)/shard_map/ppermute | solution.py:282
  56.2 6.4 %copy-start.3 = (bf16[8,256,384]{2,1,0:T(8,128)(2,1)}, bf16[8,256,384]{2,1,0:T(8,128)(2,1)S(1)}, u32[]{:S(2)}) copy-start(bf16[8,256,384]{2,1,0:T(8,128)(2,1)S(1)} %all-to-all-done.1.x_ref) | copy-start | bytes 4718596
  57.7 24.3 %all-to-all-start.2 = ((bf16[16,128,384]{2,1,0:T(8,128)(2,1)}), bf16[16,128,384]{2,1,0:T(8,128)(2,1)S(1)}, u32[]{:S(2)}, u32[]{:S(2)}) async-start(bf16[16,128,384]{2,1,0:T(8,128)(2,1)} %broadcast_in_dim.5), calls=%async_computation.2 | async-start | bytes 3145728 | tf_op jit(solution)/shard_map/all_to_all | solution.py:23
  62.6 29.2 %collective-permute-start = (bf16[8,256,384]{2,1,0:T(8,128)(2,1)S(1)}, bf16[8,256,384]{2,1,0:T(8,128)(2,1)}, u32[]{:S(2)}, u32[]{:S(2)}) collective-permute-start(bf16[8,256,384]{2,1,0:T(8,128)(2,1)S(1)} %all-to-all-done.1.x_ref), channel_id=1, source_target_pairs={{0,8},{8,0},{1,9},{9,1},{2,10},{10,2},{3,11},{11,3},{4,12},{12,4},... | collective-permute-start | bytes 4718600 | tf_op jit(solution)/shard_map/ppermute | solution.py:269
  82.0 10.7 %copy-start.4 = (bf16[16,128,384]{2,1,0:T(8,128)(2,1)}, bf16[16,128,384]{2,1,0:T(8,128)(2,1)S(1)}, u32[]{:S(2)}) copy-start(bf16[16,128,384]{2,1,0:T(8,128)(2,1)S(1)} %all-to-all-done.2) | copy-start | bytes 4718596
  82.0 9.8 %collective-permute-start.4 = (bf16[2,8,128,384]{3,2,1,0:T(8,128)(2,1)S(1)}, bf16[2,8,128,384]{3,2,1,0:T(8,128)(2,1)}, u32[]{:S(2)}, u32[]{:S(2)}) collective-permute-start(bf16[2,8,128,384]{3,2,1,0:T(8,128)(2,1)S(1)} %bitcast.7), channel_id=1, source_target_pairs={{0,8},{8,0},{1,9},{9,1},{2,10},{10,2},{3,11},{11,3},{4,12},{12,4},... | collective-permute-start | bytes 4718600 | tf_op jit(solution)/shard_map/ppermute | solution.py:269
  88.5 3.3 %collective-permute-start.5 = (s32[1,1]{1,0:T(1,128)}, s32[1,1]{1,0:T(1,128)}, u32[]{:S(2)}, u32[]{:S(2)}) collective-permute-start(s32[1,1]{1,0:T(1,128)} %param.13), channel_id=1, source_target_pairs={{0,8},{8,0},{1,9},{9,1},{2,10},{10,2},{3,11},{11,3},{4,12},{12,4},... | collective-permute-start | bytes 20 | tf_op jit(solution)/shard_map/ppermute | solution.py:269
  100.5 11.8 %copy-start = (bf16[768,256]{1,0:T(8,128)(2,1)S(1)}, bf16[768,256]{1,0:T(8,128)(2,1)}, u32[]{:S(2)}) copy-start(bf16[768,256]{1,0:T(8,128)(2,1)} %get-tuple-element.34.forward_ref) | copy-start | bytes 1179652
  100.5 14.4 %copy-start.1 = (bf16[768,256]{1,0:T(8,128)(2,1)S(1)}, bf16[768,256]{1,0:T(8,128)(2,1)}, u32[]{:S(2)}) copy-start(bf16[768,256]{1,0:T(8,128)(2,1)} %get-tuple-element.35.backward_ref) | copy-start | bytes 1179652
  100.6 20.7 %copy-start.7 = (bf16[256,256]{1,0:T(8,128)(2,1)S(1)}, bf16[256,256]{1,0:T(8,128)(2,1)}, u32[]{:S(2)}) copy-start(bf16[256,256]{1,0:T(8,128)(2,1)} %get-tuple-element.36) | copy-start | bytes 393220
  100.6 22.6 %copy-start.6 = (bf16[256,256]{1,0:T(8,128)(2,1)S(1)}, bf16[256,256]{1,0:T(8,128)(2,1)}, u32[]{:S(2)}) copy-start(bf16[256,256]{1,0:T(8,128)(2,1)} %get-tuple-element.37) | copy-start | bytes 393220
  100.6 34.4 %copy-start.2 = (bf16[2,256,128]{2,1,0:T(8,128)(2,1)S(1)}, bf16[2,256,128]{2,1,0:T(8,128)(2,1)}, u32[]{:S(2)}) copy-start(bf16[2,256,128]{2,1,0:T(8,128)(2,1)} %get-tuple-element.33.q_ref) | copy-start | bytes 393220
  101.9 41.1 %collective-permute-start.11 = (bf16[3072,128]{1,0:T(8,128)(2,1)S(1)}, bf16[3072,128]{1,0:T(8,128)(2,1)S(1)}, u32[]{:S(2)}, u32[]{:S(2)}) collective-permute-start(bf16[3072,128]{1,0:T(8,128)(2,1)S(1)} %slice.3.wx_ref), channel_id=1, source_target_pairs={{0,8},{8,0},{1,9},{9,1},{2,10},{10,2},{3,11},{11,3},{4,12},{12,4},... | collective-permute-start | bytes 2359304 | tf_op jit(solution)/shard_map/ppermute | solution.py:269
  112.3 22.7 %collective-permute-start.6 = (bf16[768,256]{1,0:T(8,128)(2,1)S(1)}, bf16[768,256]{1,0:T(8,128)(2,1)S(1)}, u32[]{:S(2)}, u32[]{:S(2)}) collective-permute-start(bf16[768,256]{1,0:T(8,128)(2,1)S(1)} %copy-done), channel_id=1, source_target_pairs={{0,16},{16,32},{32,48},{48,64},{64,80},{80,96},{96,112},{112,128},... | collective-permute-start | bytes 1179656 | tf_op jit(solution)/shard_map/ppermute | solution.py:282
  115.0 20.1 %collective-permute-start.7 = (bf16[768,256]{1,0:T(8,128)(2,1)S(1)}, bf16[768,256]{1,0:T(8,128)(2,1)S(1)}, u32[]{:S(2)}, u32[]{:S(2)}) collective-permute-start(bf16[768,256]{1,0:T(8,128)(2,1)S(1)} %copy-done.1), channel_id=1, source_target_pairs={{0,496},{16,0},{32,16},{48,32},{64,48},{80,64},{96,80},{112,96},{1... | collective-permute-start | bytes 1179656 | tf_op jit(solution)/shard_map/ppermute | solution.py:282
  121.2 9.2 %collective-permute-start.8 = (bf16[256,256]{1,0:T(8,128)(2,1)S(1)}, bf16[256,256]{1,0:T(8,128)(2,1)S(1)}, u32[]{:S(2)}, u32[]{:S(2)}) collective-permute-start(bf16[256,256]{1,0:T(8,128)(2,1)S(1)} %copy-done.7), channel_id=1, source_target_pairs={{0,32},{16,48},{32,64},{48,80},{64,96},{80,112},{96,128},{112,144}... | collective-permute-start | bytes 393224 | tf_op jit(solution)/shard_map/ppermute | solution.py:282
  123.2 11.8 %collective-permute-start.9 = (bf16[256,256]{1,0:T(8,128)(2,1)S(1)}, bf16[256,256]{1,0:T(8,128)(2,1)S(1)}, u32[]{:S(2)}, u32[]{:S(2)}) collective-permute-start(bf16[256,256]{1,0:T(8,128)(2,1)S(1)} %copy-done.6), channel_id=1, source_target_pairs={{0,224},{16,240},{32,0},{48,16},{64,32},{80,48},{96,64},{112,80},{... | collective-permute-start | bytes 393224 | tf_op jit(solution)/shard_map/ppermute | solution.py:282
  139.0 3.9 %collective-permute-start.10 = (bf16[256,128]{1,0:T(8,128)(2,1)S(1)}, bf16[256,128]{1,0:T(8,128)(2,1)S(1)}, u32[]{:S(2)}, u32[]{:S(2)}) collective-permute-start(bf16[256,128]{1,0:T(8,128)(2,1)S(1)} %get-tuple-element.39), channel_id=1, source_target_pairs={{0,8},{8,0},{1,9},{9,1},{2,10},{10,2},{3,11},{11,3},{4,12},{12,4},... | collective-permute-start | bytes 196616 | tf_op jit(solution)/shard_map/ppermute | solution.py:269
Sparse Core Ops, SparseCore 0:
  25.2 67.4 all-gather.1

commit v4 on v3

--- a/solution.py
+++ b/solution.py
@@ -65,97 +65,89 @@
     q_ref,
     acc,
     qacc,
+    tokens,
     weights,
     arrived,
 ):
-    step = pl.program_id(0)
-    pieces, count, width = x_ref.shape
+    steps, total, wide = tokens.shape
+    _, count, width = x_ref.shape
     groups, _, rows, _ = sx_ref.shape
-
-    def fetch(i):
-        lines = pl.ds(i * pieces * width, pieces * width)
-        return pltpu.make_async_copy(
-            w_ref.at[lines, pl.ds(0, 3 * HEAD)], weights.at[i], arrived.at[i]
+    pieces = wide // width
+    far = total - 2 * count
+
+    def fetches(step):
+        sources = [(r, (), count) for r in (x_ref, y_ref)]
+        sources += [(r, (g,), rows) for r in (sx_ref, sy_ref) for g in range(groups)]
+        found = [(w_ref.at[pl.ds(step * wide, wide), pl.ds(0, 3 * HEAD)], weights.at[step])]
+        for j in range(pieces):
+            at = 0
+            for r, i, n in sources:
+                lines, lanes = pl.ds(at, n), pl.ds(j * width, width)
+                found.append((r.at[i + (step * pieces + j,)], tokens.at[step, lines, lanes]))
+                at += n
+        return [
+            pltpu.make_async_copy(a, b, arrived.at[step, n]) for n, (a, b) in enumerate(found)
+        ]
+
+    for step in range(steps):
+        for copy in fetches(step):
+            copy.start()
+    acc[...] = jnp.zeros_like(acc)
+    qacc[...] = jnp.zeros_like(qacc)
+
+    @pl.loop(0, steps)
+    def _(step):
+        for copy in fetches(step):
+            copy.wait()
+        w = weights[step]
+        acc[...] += jnp.dot(tokens[step], w[:, : 2 * HEAD], preferred_element_type=F32)
+        qacc[...] += jnp.dot(
+            tokens[step, : 2 * count], w[:, 2 * HEAD :], preferred_element_type=F32
         )
 
-    @pl.when(step == 0)
-    def _():
-        for i in range(weights.shape[0]):
-            fetch(i).start()
-        acc[...] = jnp.zeros_like(acc)
-        qacc[...] = jnp.zeros_like(qacc)
-
-    fetch(step).wait()
-    w = weights[step]
-    tokens = [(t_ref, ()) for t_ref in (x_ref, y_ref)]
-    tokens += [(s_ref, (g,)) for s_ref in (sx_ref, sy_ref) for g in range(groups)]
-    t = jnp.concatenate(
-        [jnp.concatenate([r[i + (j,)] for j in range(pieces)], axis=1) for r, i in tokens], axis=0
-    )
-    acc[...] += jnp.dot(t, w[:, : 2 * HEAD], preferred_element_type=F32)
-    qacc[...] += jnp.dot(t[: 2 * count], w[:, 2 * HEAD :], preferred_element_type=F32)
-
-    @pl.when(step == pl.num_programs(0) - 1)
-    def _():
-        kg, qg = kg_ref[...], qg_ref[...]
-        far = 2 * groups * rows
-        for half, part_ref in enumerate((low_ref, high_ref)):
-            lines = pl.ds(half * far // 2, far // 2)
-            source = pl.ds(2 * count + half * far // 2, far // 2)
-            k = unit(acc[source, :HEAD], kg).astype(BF16)
-            v = acc[source, HEAD:].astype(BF16)
-            for out_ref in (forward_ref, backward_ref):
-                out_ref[lines, :HEAD] = k
-                out_ref[lines, HEAD:] = v
-            part_ref[:, :HEAD] = k
-            part_ref[:, HEAD:] = v
-        me = me_ref[0]
-        lines = pl.ds(far, count)
-        for slab, out_ref in enumerate((backward_ref, forward_ref)):
-            mine = pl.ds(pl.multiple_of((slab ^ me) * count, count), count)
-            out_ref[lines, :HEAD] = unit(acc[mine, :HEAD], kg).astype(BF16)
-            out_ref[lines, HEAD:] = acc[mine, HEAD:].astype(BF16)
-            q_ref[slab] = unit(qacc[mine], qg).astype(BF16)
+    kg, qg = kg_ref[...], qg_ref[...]
+    for half, part_ref in enumerate((low_ref, high_ref)):
+        lines = pl.ds(half * far // 2, far // 2)
+        source = pl.ds(2 * count + half * far // 2, far // 2)
+        k = unit(acc[source, :HEAD], kg).astype(BF16)
+        v = acc[source, HEAD:].astype(BF16)
+        for out_ref in (forward_ref, backward_ref):
+            out_ref[lines, :HEAD] = k
+            out_ref[lines, HEAD:] = v
+        part_ref[:, :HEAD] = k
+        part_ref[:, HEAD:] = v
+    me = me_ref[0]
+    lines = pl.ds(far, count)
+    for slab, out_ref in enumerate((backward_ref, forward_ref)):
+        mine = pl.ds(pl.multiple_of((slab ^ me) * count, count), count)
+        out_ref[lines, :HEAD] = unit(acc[mine, :HEAD], kg).astype(BF16)
+        out_ref[lines, HEAD:] = acc[mine, HEAD:].astype(BF16)
+        q_ref[slab] = unit(qacc[mine], qg).astype(BF16)
 
 
 def project(me, slabs, styles, w, query_gain, key_gain):
     parts, count, width = slabs[0].shape
     groups, _, rows, _ = styles[0].shape
     pieces = 2
+    steps = parts // pieces
     far = 2 * groups * rows
-    slab = pl.BlockSpec((pieces, count, width), lambda i: (i, 0, 0))
-    style = pl.BlockSpec((groups, pieces, rows, width), lambda i: (0, i, 0, 0))
-    gain = pl.BlockSpec((1, HEAD), lambda i: (0, 0))
-
-    def out(*shape):
-        spec = pl.BlockSpec(shape, lambda i: (0,) * len(shape))
-        return spec, jax.ShapeDtypeStruct(shape, BF16)
-
-    pair = (far + count, 2 * HEAD)
-    part = (far // 2, 2 * HEAD)
-    outs = [out(*pair), out(*pair), out(*part), out(*part), out(2, count, HEAD)]
+    total = 2 * count + far
+    shapes = [(far + count, 2 * HEAD)] * 2 + [(far // 2, 2 * HEAD)] * 2 + [(2, count, HEAD)]
+    vmem = pl.BlockSpec(memory_space=pltpu.VMEM)
+    hbm = pl.BlockSpec(memory_space=pltpu.HBM)
     return pl.pallas_call(
         project_kernel,
-        grid=(parts // pieces,),
-        in_specs=[
-            pl.BlockSpec(memory_space=pltpu.SMEM),
-            slab,
-            slab,
-            style,
-            style,
-            pl.BlockSpec(memory_space=pltpu.HBM),
-            gain,
-            gain,
+        in_specs=[pl.BlockSpec(memory_space=pltpu.SMEM)] + [hbm] * 5 + [vmem] * 2,
+        out_specs=[vmem] * len(shapes),
+        out_shape=[jax.ShapeDtypeStruct(shape, BF16) for shape in shapes],
+        scratch_shapes=[
+            pltpu.VMEM((total, 2 * HEAD), F32),
+            pltpu.VMEM((2 * count, HEAD), F32),
+            pltpu.VMEM((steps, total, pieces * width), BF16),
+            pltpu.VMEM((steps, pieces * width, 3 * HEAD), BF16),
+            pltpu.SemaphoreType.DMA((steps, 1 + pieces * (2 + 2 * groups))),
         ],
-        out_specs=[o[0] for o in outs],
-        out_shape=[o[1] for o in outs],
-        scratch_shapes=[
-            pltpu.VMEM((2 * count + far, 2 * HEAD), F32),
-            pltpu.VMEM((2 * count, HEAD), F32),
-            pltpu.VMEM((parts // pieces, pieces * width, 3 * HEAD), BF16),
-            pltpu.SemaphoreType.DMA((parts // pieces,)),
-        ],
-        compiler_params=pltpu.CompilerParams(vmem_limit_bytes=58 << 20),
+        compiler_params=pltpu.CompilerParams(vmem_limit_bytes=60 << 20),
         name="project",
     )(me, *slabs, *styles, w, query_gain, key_gain)
 

time: 178 us -> 177 us (level)
  no operation moved by 1% of the time
where the time goes in v4:
time: 177 us; the launch traced here: 176 us
  starting transfers between devices  72.9 us (41%)
  blocking collectives  42 us (24%)
  waiting for transfers between devices  27.2 us (15%)
  between operations  14.3 us (8%)
  Pallas kernels  13.3 us (8%)
  local copies, waits for them, and re-layouts  5.05 us (3%)
    ppermute x7, starting transfers between devices, shift(): lax.ppermute(block, axes, [(i, (i + by) % count) for i in range(count)])  37.1 us
    ppermute x5, starting transfers between devices, swap(): return lax.ppermute(block, 'core', [(0, 1), (1, 0)])  27.2 us
    all_to_all x1, blocking collectives, local(): shares = lax.all_to_all(shares, TP, 0, 0, tiled=True)  25.1 us
    all_to_all x1, blocking collectives, local(): plane = lax.all_to_all(mine, ('x_hi', 'core'), 0, 0, tiled=True)  17 us
    all_to_all x2, waiting for transfers between devices, spread(): lax.all_to_all(jnp.broadcast_to(block[None], (count,) + block.shape), axe...  14.1 us
    ppermute x7, waiting for transfers between devices, shift(): lax.ppermute(block, axes, [(i, (i + by) % count) for i in range(count)])  9.97 us
    all_to_all x2, starting transfers between devices, spread(): lax.all_to_all(jnp.broadcast_to(block[None], (count,) + block.shape), axe...  8.59 us
    pallas_call x1, Pallas kernels, project(): pl.pallas_call(project_kernel, in_specs=[pl.BlockSpec(memory_space=pltpu....  7.09 us
  transfers between devices with their start and end apart: 15, of which 7 were waited for; matrix products, arithmetic and copies ran while one was open for 2% of the time, Pallas kernels for 2%

profile of v4, /device:TPU:1, one launch (start us, length us, event | category | flops | bytes accessed | tf_op | source)
XLA Modules:
  0.0 175.8 jit_solution(11592894202814077446)
XLA Ops:
  6.5 0.0 all-gather.2.cloned.1.call-start
  6.5 1.6 pack.1
  8.1 17.0 %all_to_all.20 = bf16[4,48,512]{2,1,0:T(8,128)(2,1)} all-to-all(bf16[4,48,512]{2,1,0:T(8,128)(2,1)} %pack.1), channel_id=1, replica_groups=mesh['x_hi'=2,'z_hi'=4,'z_lo'=4,'core'=2,'y'=4,'x_lo'=2] {'x_hi','core'}, dimensions={0} | all-to-all | bytes 393216 | tf_op jit(solution)/shard_map/all_to_all | solution.py:265
  25.1 0.0 all-gather.2.cloned.1.call-update
  25.1 2.2 %broadcast_in_dim.4 = bf16[8,256,384]{2,1,0:T(8,128)(2,1)} broadcast(bf16[256,384]{1,0:T(8,128)(2,1)} %param.7), dimensions={1,2} | broadcast | bytes 1769472 | tf_op jit(solution)/shard_map/broadcast_in_dim | solution.py:24
  27.3 3.7 %all-to-all-start.1 = ((bf16[8,256,384]{2,1,0:T(8,128)(2,1)}), bf16[8,256,384]{2,1,0:T(8,128)(2,1)S(1)}, u32[]{:S(2)}, u32[]{:S(2)}) async-start(bf16[8,256,384]{2,1,0:T(8,128)(2,1)} %broadcast_in_dim.4), calls=%async_computation.1 | async-start | bytes 3145728 | tf_op jit(solution)/shard_map/all_to_all | solution.py:23
  31.1 0.0 copy-done.5
  31.1 5.0 %collective-permute-start.1 = (bf16[32,384]{1,0:T(8,128)(2,1)S(1)}, bf16[32,384]{1,0:T(8,128)(2,1)S(1)}, u32[]{:S(2)}, u32[]{:S(2)}) collective-permute-start(bf16[32,384]{1,0:T(8,128)(2,1)S(1)} %copy-done.5), channel_id=1, source_target_pairs={{0,64},{16,80},{32,96},{48,112},{64,128},{80,144},{96,160},{112,17... | collective-permute-start | bytes 73736 | tf_op jit(solution)/shard_map/ppermute | solution.py:274
  36.1 10.6 %collective-permute-start.2 = (bf16[32,384]{1,0:T(8,128)(2,1)S(1)}, bf16[32,384]{1,0:T(8,128)(2,1)S(1)}, u32[]{:S(2)}, u32[]{:S(2)}) collective-permute-start(bf16[32,384]{1,0:T(8,128)(2,1)S(1)} %copy-done.5), channel_id=1, source_target_pairs={{0,128},{16,144},{32,160},{48,176},{64,192},{80,208},{96,224},{112... | collective-permute-start | bytes 73736 | tf_op jit(solution)/shard_map/ppermute | solution.py:274
  46.7 5.2 %collective-permute-start.3 = (bf16[32,384]{1,0:T(8,128)(2,1)S(1)}, bf16[32,384]{1,0:T(8,128)(2,1)S(1)}, u32[]{:S(2)}, u32[]{:S(2)}) collective-permute-start(bf16[32,384]{1,0:T(8,128)(2,1)S(1)} %copy-done.5), channel_id=1, source_target_pairs={{0,192},{16,208},{32,224},{48,240},{64,0},{80,16},{96,32},{112,48}... | collective-permute-start | bytes 73736 | tf_op jit(solution)/shard_map/ppermute | solution.py:274
  51.9 0.0 collective-permute-done.1
  51.9 0.0 collective-permute-done.2
  51.9 4.3 %collective-permute-done.3 = bf16[32,384]{1,0:T(8,128)(2,1)S(1)} collective-permute-done((bf16[32,384]{1,0:T(8,128)(2,1)S(1)}, bf16[32,384]{1,0:T(8,128)(2,1)S(1)}, u32[]{:S(2)}, u32[]{:S(2)}) %collective-permute-start.3) | collective-permute-done | bytes 24608 | tf_op jit(solution)/shard_map/ppermute | solution.py:274
  56.2 0.0 all-to-all-done.1.x_ref
  56.2 0.0 copy-start.3
  56.2 1.5 broadcast_in_dim.5
  57.7 4.9 %all-to-all-start.2 = ((bf16[16,128,384]{2,1,0:T(8,128)(2,1)}), bf16[16,128,384]{2,1,0:T(8,128)(2,1)S(1)}, u32[]{:S(2)}, u32[]{:S(2)}) async-start(bf16[16,128,384]{2,1,0:T(8,128)(2,1)} %broadcast_in_dim.5), calls=%async_computation.2 | async-start | bytes 3145728 | tf_op jit(solution)/shard_map/all_to_all | solution.py:23
  62.6 0.0 copy-done.3
  62.6 5.3 %collective-permute-start = (bf16[8,256,384]{2,1,0:T(8,128)(2,1)S(1)}, bf16[8,256,384]{2,1,0:T(8,128)(2,1)}, u32[]{:S(2)}, u32[]{:S(2)}) collective-permute-start(bf16[8,256,384]{2,1,0:T(8,128)(2,1)S(1)} %all-to-all-done.1.x_ref), channel_id=1, source_target_pairs={{0,8},{8,0},{1,9},{9,1},{2,10},{10,2},{3,11},{11,3},{4,12},{12,4},... | collective-permute-start | bytes 4718600 | tf_op jit(solution)/shard_map/ppermute | solution.py:261
  67.9 14.1 %all-to-all-done.2 = bf16[16,128,384]{2,1,0:T(8,128)(2,1)S(1)} async-done(((bf16[16,128,384]{2,1,0:T(8,128)(2,1)}), bf16[16,128,384]{2,1,0:T(8,128)(2,1)S(1)}, u32[]{:S(2)}, u32[]{:S(2)}) %all-to-all-start.2) | async-done | bytes 1572896 | tf_op jit(solution)/shard_map/all_to_all | solution.py:23
  82.0 6.5 %collective-permute-start.4 = (bf16[2,8,128,384]{3,2,1,0:T(8,128)(2,1)S(1)}, bf16[2,8,128,384]{3,2,1,0:T(8,128)(2,1)}, u32[]{:S(2)}, u32[]{:S(2)}) collective-permute-start(bf16[2,8,128,384]{3,2,1,0:T(8,128)(2,1)S(1)} %bitcast.7), channel_id=1, source_target_pairs={{0,8},{8,0},{1,9},{9,1},{2,10},{10,2},{3,11},{11,3},{4,12},{12,4},... | collective-permute-start | bytes 4718600 | tf_op jit(solution)/shard_map/ppermute | solution.py:261
  88.5 1.9 %collective-permute-start.5 = (s32[1,1]{1,0:T(1,128)}, s32[1,1]{1,0:T(1,128)}, u32[]{:S(2)}, u32[]{:S(2)}) collective-permute-start(s32[1,1]{1,0:T(1,128)} %param.13), channel_id=1, source_target_pairs={{0,8},{8,0},{1,9},{9,1},{2,10},{10,2},{3,11},{11,3},{4,12},{12,4},... | collective-permute-start | bytes 20 | tf_op jit(solution)/shard_map/ppermute | solution.py:261
  90.5 1.4 collective-permute-done.5.fy_ref
  91.8 0.0 collective-permute-done.y_ref
  91.8 0.0 collective-permute-done.4.sy_ref
  91.8 0.9 all-gather.2.cloned.1.call-done
  92.7 0.0 copy-done.4
  92.7 7.1 %project.1 = (bf16[768,256]{1,0:T(8,128)(2,1)}, bf16[768,256]{1,0:T(8,128)(2,1)}, bf16[256,256]{1,0:T(8,128)(2,1)}, bf16[256,256]{1,0:T(8,128)(2,1)}, bf16[2,256,128]{2,1,0:T(8,128)(2,1)}) custom-call(s32[1]{0:T(128)} %bitcast.me_ref, bf16[8,256,384]{2,1,0:T(8,128)(2,1)} %copy-done.3, bf16[8,256,384]{2,1,0:T(8,128)(2,1)} %collective-permute-done.y_ref, ...), custom_call_target="tpu_custom_call" | custom-call | tf_op jit(solution)/shard_map/project/pallas_call | solution.py:138
  99.9 0.0 copy-start.7
  99.9 0.0 copy-start.6
  99.9 0.0 copy-start.2
  99.9 1.3 slice.3.wx_ref
  101.2 10.4 %collective-permute-start.11 = (bf16[3072,128]{1,0:T(8,128)(2,1)S(1)}, bf16[3072,128]{1,0:T(8,128)(2,1)S(1)}, u32[]{:S(2)}, u32[]{:S(2)}) collective-permute-start(bf16[3072,128]{1,0:T(8,128)(2,1)S(1)} %slice.3.wx_ref), channel_id=1, source_target_pairs={{0,8},{8,0},{1,9},{9,1},{2,10},{10,2},{3,11},{11,3},{4,12},{12,4},... | collective-permute-start | bytes 2359304 | tf_op jit(solution)/shard_map/ppermute | solution.py:261
  111.6 2.6 %collective-permute-start.6 = (bf16[768,256]{1,0:T(8,128)(2,1)S(1)}, bf16[768,256]{1,0:T(8,128)(2,1)S(1)}, u32[]{:S(2)}, u32[]{:S(2)}) collective-permute-start(bf16[768,256]{1,0:T(8,128)(2,1)S(1)} %copy-done), channel_id=1, source_target_pairs={{0,16},{16,32},{32,48},{48,64},{64,80},{80,96},{96,112},{112,128},... | collective-permute-start | bytes 1179656 | tf_op jit(solution)/shard_map/ppermute | solution.py:274
  114.3 6.3 %collective-permute-start.7 = (bf16[768,256]{1,0:T(8,128)(2,1)S(1)}, bf16[768,256]{1,0:T(8,128)(2,1)S(1)}, u32[]{:S(2)}, u32[]{:S(2)}) collective-permute-start(bf16[768,256]{1,0:T(8,128)(2,1)S(1)} %copy-done.1), channel_id=1, source_target_pairs={{0,496},{16,0},{32,16},{48,32},{64,48},{80,64},{96,80},{112,96},{1... | collective-permute-start | bytes 1179656 | tf_op jit(solution)/shard_map/ppermute | solution.py:274
  120.5 1.9 %collective-permute-start.8 = (bf16[256,256]{1,0:T(8,128)(2,1)S(1)}, bf16[256,256]{1,0:T(8,128)(2,1)S(1)}, u32[]{:S(2)}, u32[]{:S(2)}) collective-permute-start(bf16[256,256]{1,0:T(8,128)(2,1)S(1)} %copy-done.7), channel_id=1, source_target_pairs={{0,32},{16,48},{32,64},{48,80},{64,96},{80,112},{96,128},{112,144}... | collective-permute-start | bytes 393224 | tf_op jit(solution)/shard_map/ppermute | solution.py:274
  122.5 5.5 %collective-permute-start.9 = (bf16[256,256]{1,0:T(8,128)(2,1)S(1)}, bf16[256,256]{1,0:T(8,128)(2,1)S(1)}, u32[]{:S(2)}, u32[]{:S(2)}) collective-permute-start(bf16[256,256]{1,0:T(8,128)(2,1)S(1)} %copy-done.6), channel_id=1, source_target_pairs={{0,224},{16,240},{32,0},{48,16},{64,32},{80,48},{96,64},{112,80},{... | collective-permute-start | bytes 393224 | tf_op jit(solution)/shard_map/ppermute | solution.py:274
  128.6 1.2 collective-permute-done.8.low_ref
  129.8 4.5 %collective-permute-done.9.high_ref = bf16[256,256]{1,0:T(8,128)(2,1)S(1)} collective-permute-done((bf16[256,256]{1,0:T(8,128)(2,1)S(1)}, bf16[256,256]{1,0:T(8,128)(2,1)S(1)}, u32[]{:S(2)}, u32[]{:S(2)}) %collective-permute-start.9) | collective-permute-done | bytes 131104 | tf_op jit(solution)/shard_map/ppermute | solution.py:274
  134.3 0.0 collective-permute-done.6.before_ref
  134.3 0.0 collective-permute-done.7.after_ref
  134.3 4.0 %attend.1 = (bf16[256,128]{1,0:T(8,128)(2,1)S(1)}, bf16[256,128]{1,0:T(8,128)(2,1)S(1)}) custom-call(s32[1]{0:T(128)} %bitcast.me_ref, s32[1,1]{1,0:T(1,128)S(6)} %copy.8.fx_ref, s32[1,1]{1,0:T(1,128)} %collective-permute-done.5.fy_ref, bf16[2,256,128]{2,1,0:T(8,128)(2,1)S(1)} %copy-done.2, bf16[768,256]{1,0:T(8,128)(2,1)S(1)} %copy-done, ...), custom_call_target="tpu_custom_call" | custom-call | tf_op jit(solution)/shard_map/attend/pallas_call | solution.py:219
  138.3 3.1 %collective-permute-start.10 = (bf16[256,128]{1,0:T(8,128)(2,1)S(1)}, bf16[256,128]{1,0:T(8,128)(2,1)S(1)}, u32[]{:S(2)}, u32[]{:S(2)}) collective-permute-start(bf16[256,128]{1,0:T(8,128)(2,1)S(1)} %get-tuple-element.39), channel_id=1, source_target_pairs={{0,8},{8,0},{1,9},{9,1},{2,10},{10,2},{3,11},{11,3},{4,12},{12,4},... | collective-permute-start | bytes 196616 | tf_op jit(solution)/shard_map/ppermute | solution.py:261
  141.4 0.9 collective-permute-done.10.ay_ref
  142.2 0.0 collective-permute-done.11.wy_ref
  142.2 0.7 mix.1
  143.0 25.1 %all_to_all.21 = bf16[8,256,384]{2,1,0:T(8,128)(2,1)S(1)} all-to-all(bf16[8,256,384]{2,1,0:T(8,128)(2,1)S(1)} %mix.1), channel_id=1, replica_groups=mesh['x_hi'=2,'z_hi'=4,'z_lo'=4,'core'=2,'y'=4,'x_lo'=2] {'y','x_lo'}, dimensions={0} | all-to-all | bytes 3145728 | tf_op jit(solution)/shard_map/all_to_all | solution.py:302
  168.0 0.9 reduce_sum.12
  (10 shorter events, 0.0 us)
Async XLA Ops:
  6.5 86.2 %all-gather.2.cloned.1.call-start = ((), (), s32[]{:S(2)}) async-start(), calls=%async_computation.4 | async-start | bytes 3342336 | tf_op jit(solution)/shard_map/all_gather | solution.py:267
  27.3 3.7 %copy-start.5 = (bf16[32,384]{1,0:T(8,128)(2,1)S(1)}, bf16[32,384]{1,0:T(8,128)(2,1)}, u32[]{:S(2)}) copy-start(bf16[32,384]{1,0:T(8,128)(2,1)} %param.8) | copy-start | bytes 73732
  27.3 28.9 %all-to-all-start.1 = ((bf16[8,256,384]{2,1,0:T(8,128)(2,1)}), bf16[8,256,384]{2,1,0:T(8,128)(2,1)S(1)}, u32[]{:S(2)}, u32[]{:S(2)}) async-start(bf16[8,256,384]{2,1,0:T(8,128)(2,1)} %broadcast_in_dim.4), calls=%async_computation.1 | async-start | bytes 3145728 | tf_op jit(solution)/shard_map/all_to_all | solution.py:23
  31.1 20.8 %collective-permute-start.1 = (bf16[32,384]{1,0:T(8,128)(2,1)S(1)}, bf16[32,384]{1,0:T(8,128)(2,1)S(1)}, u32[]{:S(2)}, u32[]{:S(2)}) collective-permute-start(bf16[32,384]{1,0:T(8,128)(2,1)S(1)} %copy-done.5), channel_id=1, source_target_pairs={{0,64},{16,80},{32,96},{48,112},{64,128},{80,144},{96,160},{112,17... | collective-permute-start | bytes 73736 | tf_op jit(solution)/shard_map/ppermute | solution.py:274
  36.1 15.8 %collective-permute-start.2 = (bf16[32,384]{1,0:T(8,128)(2,1)S(1)}, bf16[32,384]{1,0:T(8,128)(2,1)S(1)}, u32[]{:S(2)}, u32[]{:S(2)}) collective-permute-start(bf16[32,384]{1,0:T(8,128)(2,1)S(1)} %copy-done.5), channel_id=1, source_target_pairs={{0,128},{16,144},{32,160},{48,176},{64,192},{80,208},{96,224},{112... | collective-permute-start | bytes 73736 | tf_op jit(solution)/shard_map/ppermute | solution.py:274
  46.7 9.5 %collective-permute-start.3 = (bf16[32,384]{1,0:T(8,128)(2,1)S(1)}, bf16[32,384]{1,0:T(8,128)(2,1)S(1)}, u32[]{:S(2)}, u32[]{:S(2)}) collective-permute-start(bf16[32,384]{1,0:T(8,128)(2,1)S(1)} %copy-done.5), channel_id=1, source_target_pairs={{0,192},{16,208},{32,224},{48,240},{64,0},{80,16},{96,32},{112,48}... | collective-permute-start | bytes 73736 | tf_op jit(solution)/shard_map/ppermute | solution.py:274
  56.2 6.4 %copy-start.3 = (bf16[8,256,384]{2,1,0:T(8,128)(2,1)}, bf16[8,256,384]{2,1,0:T(8,128)(2,1)S(1)}, u32[]{:S(2)}) copy-start(bf16[8,256,384]{2,1,0:T(8,128)(2,1)S(1)} %all-to-all-done.1.x_ref) | copy-start | bytes 4718596
  57.7 24.3 %all-to-all-start.2 = ((bf16[16,128,384]{2,1,0:T(8,128)(2,1)}), bf16[16,128,384]{2,1,0:T(8,128)(2,1)S(1)}, u32[]{:S(2)}, u32[]{:S(2)}) async-start(bf16[16,128,384]{2,1,0:T(8,128)(2,1)} %broadcast_in_dim.5), calls=%async_computation.2 | async-start | bytes 3145728 | tf_op jit(solution)/shard_map/all_to_all | solution.py:23
  62.6 29.2 %collective-permute-start = (bf16[8,256,384]{2,1,0:T(8,128)(2,1)S(1)}, bf16[8,256,384]{2,1,0:T(8,128)(2,1)}, u32[]{:S(2)}, u32[]{:S(2)}) collective-permute-start(bf16[8,256,384]{2,1,0:T(8,128)(2,1)S(1)} %all-to-all-done.1.x_ref), channel_id=1, source_target_pairs={{0,8},{8,0},{1,9},{9,1},{2,10},{10,2},{3,11},{11,3},{4,12},{12,4},... | collective-permute-start | bytes 4718600 | tf_op jit(solution)/shard_map/ppermute | solution.py:261
  82.0 10.7 %copy-start.4 = (bf16[16,128,384]{2,1,0:T(8,128)(2,1)}, bf16[16,128,384]{2,1,0:T(8,128)(2,1)S(1)}, u32[]{:S(2)}) copy-start(bf16[16,128,384]{2,1,0:T(8,128)(2,1)S(1)} %all-to-all-done.2) | copy-start | bytes 4718596
  82.0 9.8 %collective-permute-start.4 = (bf16[2,8,128,384]{3,2,1,0:T(8,128)(2,1)S(1)}, bf16[2,8,128,384]{3,2,1,0:T(8,128)(2,1)}, u32[]{:S(2)}, u32[]{:S(2)}) collective-permute-start(bf16[2,8,128,384]{3,2,1,0:T(8,128)(2,1)S(1)} %bitcast.7), channel_id=1, source_target_pairs={{0,8},{8,0},{1,9},{9,1},{2,10},{10,2},{3,11},{11,3},{4,12},{12,4},... | collective-permute-start | bytes 4718600 | tf_op jit(solution)/shard_map/ppermute | solution.py:261
  88.5 3.3 %collective-permute-start.5 = (s32[1,1]{1,0:T(1,128)}, s32[1,1]{1,0:T(1,128)}, u32[]{:S(2)}, u32[]{:S(2)}) collective-permute-start(s32[1,1]{1,0:T(1,128)} %param.13), channel_id=1, source_target_pairs={{0,8},{8,0},{1,9},{9,1},{2,10},{10,2},{3,11},{11,3},{4,12},{12,4},... | collective-permute-start | bytes 20 | tf_op jit(solution)/shard_map/ppermute | solution.py:261
  99.8 11.8 %copy-start = (bf16[768,256]{1,0:T(8,128)(2,1)S(1)}, bf16[768,256]{1,0:T(8,128)(2,1)}, u32[]{:S(2)}) copy-start(bf16[768,256]{1,0:T(8,128)(2,1)} %get-tuple-element.34.forward_ref) | copy-start | bytes 1179652
  99.9 14.4 %copy-start.1 = (bf16[768,256]{1,0:T(8,128)(2,1)S(1)}, bf16[768,256]{1,0:T(8,128)(2,1)}, u32[]{:S(2)}) copy-start(bf16[768,256]{1,0:T(8,128)(2,1)} %get-tuple-element.35.backward_ref) | copy-start | bytes 1179652
  99.9 20.7 %copy-start.7 = (bf16[256,256]{1,0:T(8,128)(2,1)S(1)}, bf16[256,256]{1,0:T(8,128)(2,1)}, u32[]{:S(2)}) copy-start(bf16[256,256]{1,0:T(8,128)(2,1)} %get-tuple-element.36) | copy-start | bytes 393220
  99.9 22.6 %copy-start.6 = (bf16[256,256]{1,0:T(8,128)(2,1)S(1)}, bf16[256,256]{1,0:T(8,128)(2,1)}, u32[]{:S(2)}) copy-start(bf16[256,256]{1,0:T(8,128)(2,1)} %get-tuple-element.37) | copy-start | bytes 393220
  99.9 34.4 %copy-start.2 = (bf16[2,256,128]{2,1,0:T(8,128)(2,1)S(1)}, bf16[2,256,128]{2,1,0:T(8,128)(2,1)}, u32[]{:S(2)}) copy-start(bf16[2,256,128]{2,1,0:T(8,128)(2,1)} %get-tuple-element.33.q_ref) | copy-start | bytes 393220
  101.2 41.1 %collective-permute-start.11 = (bf16[3072,128]{1,0:T(8,128)(2,1)S(1)}, bf16[3072,128]{1,0:T(8,128)(2,1)S(1)}, u32[]{:S(2)}, u32[]{:S(2)}) collective-permute-start(bf16[3072,128]{1,0:T(8,128)(2,1)S(1)} %slice.3.wx_ref), channel_id=1, source_target_pairs={{0,8},{8,0},{1,9},{9,1},{2,10},{10,2},{3,11},{11,3},{4,12},{12,4},... | collective-permute-start | bytes 2359304 | tf_op jit(solution)/shard_map/ppermute | solution.py:261
  111.6 22.7 %collective-permute-start.6 = (bf16[768,256]{1,0:T(8,128)(2,1)S(1)}, bf16[768,256]{1,0:T(8,128)(2,1)S(1)}, u32[]{:S(2)}, u32[]{:S(2)}) collective-permute-start(bf16[768,256]{1,0:T(8,128)(2,1)S(1)} %copy-done), channel_id=1, source_target_pairs={{0,16},{16,32},{32,48},{48,64},{64,80},{80,96},{96,112},{112,128},... | collective-permute-start | bytes 1179656 | tf_op jit(solution)/shard_map/ppermute | solution.py:274
  114.3 20.1 %collective-permute-start.7 = (bf16[768,256]{1,0:T(8,128)(2,1)S(1)}, bf16[768,256]{1,0:T(8,128)(2,1)S(1)}, u32[]{:S(2)}, u32[]{:S(2)}) collective-permute-start(bf16[768,256]{1,0:T(8,128)(2,1)S(1)} %copy-done.1), channel_id=1, source_target_pairs={{0,496},{16,0},{32,16},{48,32},{64,48},{80,64},{96,80},{112,96},{1... | collective-permute-start | bytes 1179656 | tf_op jit(solution)/shard_map/ppermute | solution.py:274
  120.5 9.2 %collective-permute-start.8 = (bf16[256,256]{1,0:T(8,128)(2,1)S(1)}, bf16[256,256]{1,0:T(8,128)(2,1)S(1)}, u32[]{:S(2)}, u32[]{:S(2)}) collective-permute-start(bf16[256,256]{1,0:T(8,128)(2,1)S(1)} %copy-done.7), channel_id=1, source_target_pairs={{0,32},{16,48},{32,64},{48,80},{64,96},{80,112},{96,128},{112,144}... | collective-permute-start | bytes 393224 | tf_op jit(solution)/shard_map/ppermute | solution.py:274
  122.5 11.8 %collective-permute-start.9 = (bf16[256,256]{1,0:T(8,128)(2,1)S(1)}, bf16[256,256]{1,0:T(8,128)(2,1)S(1)}, u32[]{:S(2)}, u32[]{:S(2)}) collective-permute-start(bf16[256,256]{1,0:T(8,128)(2,1)S(1)} %copy-done.6), channel_id=1, source_target_pairs={{0,224},{16,240},{32,0},{48,16},{64,32},{80,48},{96,64},{112,80},{... | collective-permute-start | bytes 393224 | tf_op jit(solution)/shard_map/ppermute | solution.py:274
  138.3 4.0 %collective-permute-start.10 = (bf16[256,128]{1,0:T(8,128)(2,1)S(1)}, bf16[256,128]{1,0:T(8,128)(2,1)S(1)}, u32[]{:S(2)}, u32[]{:S(2)}) collective-permute-start(bf16[256,128]{1,0:T(8,128)(2,1)S(1)} %get-tuple-element.39), channel_id=1, source_target_pairs={{0,8},{8,0},{1,9},{9,1},{2,10},{10,2},{3,11},{11,3},{4,12},{12,4},... | collective-permute-start | bytes 196616 | tf_op jit(solution)/shard_map/ppermute | solution.py:261
Sparse Core Ops, SparseCore 0:
  25.2 67.4 all-gather.1
